TPU v7x, 32 devices: a whole 2x2x4 slice. The times are simulated.
32 devices in a mesh: grp: 2 (over x), lat: 8 (over z, y), lon: 2 (over core).
Axes of the slice: x: 2, y: 2, z: 4, core: 2. Of those that a mesh axis runs over, the one named last changes fastest.
Arguments:
- fields: bfloat16 [4, 128, 384, 256], P('grp', 'lat', 'lon'), parts along dimension 0
- mix_gain: float32 [2, 256], replicated, may hold values from 0.1 to 1.9
- lat_weight: bfloat16 [2, 5, 2, 128, 128], replicated, may hold values from -0.25 to 0.25
- lon_weight: bfloat16 [2, 5, 2, 128, 128], replicated, may hold values from -0.25 to 0.25
- mlp_gain: float32 [256], replicated, may hold values from 0.1 to 1.9
- w_in: bfloat16 [256, 1024], replicated, may hold values from -0.375 to 0.375
- w_out: bfloat16 [1024, 256], replicated, may hold values from -0.1875 to 0.1875
- lat_dilation: int32 [2], replicated, may hold values from 1 to 4, as said below
- lon_dilation: int32 [2], replicated, may hold values from 1 to 24, as said below
- ocean: int32 [256, 384], P(('grp', 'lat'), 'lon'), parts along dimension 0, may hold values 0 or 1
Outputs:
- mixed: bfloat16 [4, 128, 384, 256], P('grp', 'lat', 'lon'), parts along dimension 0
There are 2 independent parts, one for each index of `grp`. A program takes and returns all parts, laid end to end along the dimension named above; an argument that names none is the same for every part. Nothing has to cross between parts.
Inputs may be any that keep to these rules, and one draw needn't show every extreme that they name: `lat_dilation`: 4 is taken by exactly one layer in every draw. `lon_dilation`: 24 is taken by exactly one layer in every draw.
All inputs are finite; a program needn't handle non-finite values. No bound on the sum of `ocean` on one device may be relied on, other than what follows from the above.
Results may differ from a plain program's by a relative error of at most 0.0075.
Values may be sent and summed in bfloat16 or wider, within the bound.
A program may use at most 128 MiB of HBM per device.

v0:
```python
import functools

import jax
import jax.numpy as jnp
from jax import lax
from jax.experimental import pallas as pl
from jax.experimental.pallas import tpu as pltpu
from jax.sharding import PartitionSpec as P

C = 256
GROUPS = 2
CG = 128
TAPS = 5
HALF = 2
LAYERS = 2
MAXDIL_LAT = 4
MAXDIL_LON = 24
REACH = HALF * MAXDIL_LAT
LON_REACH = HALF * MAXDIL_LON
TILE_COLS = LON_REACH
TILE_ROWS = 4
VMEM_LIMIT = 48 * 1024 * 1024


def scaled(wide, gain):
    power = jnp.mean(wide * wide, axis=-1, keepdims=True)
    return wide * lax.rsqrt(power + 1e-06) * gain


def block_diagonal(weight):
    zero = jnp.zeros_like(weight[:, 0])
    top = jnp.concatenate([weight[:, 0], zero], -1)
    low = jnp.concatenate([zero, weight[:, 1]], -1)
    return jnp.concatenate([top, low], -2).reshape(TAPS * C, C)


def conv_rows(held, weight_ref, dilation, first, count):
    pieces = []
    for tap in range(TAPS):
        piece = held[pl.ds(first + (tap - HALF) * dilation, count)]
        pieces.append(piece.reshape(count * held.shape[1], C))
    total = jnp.dot(
        jnp.concatenate(pieces, 1), weight_ref[...], preferred_element_type=jnp.float32
    )
    return total.astype(jnp.bfloat16).reshape(count, held.shape[1], C)


def lat_first(info, own, edge, rest, near, far, gain, weight, *refs):
    outs, held = refs[:-1], refs[-1]
    member = info[0]
    rows = own.shape[1]
    other = 1 - member
    spare = rows - REACH

    def put(ref, at, state=None):
        value = ref[...]
        size = value.shape[0]
        if state is not None:
            state[pl.ds(at - REACH, size)] = value
        held[pl.ds(at, size)] = scaled(value.astype(jnp.float32), gain[...]).astype(jnp.bfloat16)

    def work(across, state):
        put(near, other * (REACH + 2 * rows))
        put(far, member * (REACH + 2 * rows))
        put(own.at[0], REACH + member * rows, state)
        put(edge, REACH + other * (rows + spare), state)
        put(rest, REACH + other * rows + member * REACH, state)
        for part in range(2):
            across[part * rows : (part + 1) * rows] = conv_rows(
                held, weight, info[1], REACH + part * rows, rows
            )

    if len(outs) == 2:
        work(*outs)
        return

    @pl.when(pl.program_id(0) == 0)
    def _():
        work(outs[0], outs[2])

    @pl.when(pl.program_id(0) == 1)
    def _():
        work(outs[1], outs[3])


def put_ends(across, head, tail):
    step = pl.program_id(0)

    @pl.when(step == 0)
    def _():
        head[...] = across[...]

    @pl.when(step == pl.num_programs(0) - 1)
    def _():
        tail[...] = across[...]


def lat_inner(info, top, bottom, inner, weight, across, head, tail, held):
    rows = inner.shape[0]
    held[0:REACH] = top[...]
    held[REACH : REACH + rows] = inner[...]
    held[REACH + rows : 2 * REACH + rows] = bottom[...]
    across[...] = conv_rows(held, weight, info[2], REACH, rows)
    put_ends(across, head, tail)


def lat_edge(info, top, bottom, inner, north, south, weight, across, head, tail, held):
    rows = inner.shape[0]
    at = 0
    for ref in (north, top, inner, bottom, south):
        held[at : at + ref.shape[0]] = ref[...]
        at += ref.shape[0]
    across[0:REACH] = conv_rows(held, weight, info[2], REACH, REACH)
    across[REACH:] = conv_rows(held, weight, info[2], 2 * REACH + rows, REACH)
    put_ends(across, head, tail)


def lon_total(dilation, pieces, weight, wide):
    at = 0
    for piece in pieces:
        width = piece.shape[1]
        for group in range(GROUPS):
            wide[group, :, at : at + width] = piece[
                :, :, group * CG : (group + 1) * CG
            ].astype(jnp.float32)
        at += width
    cols = at - 2 * LON_REACH
    totals = []
    for row in range(TILE_ROWS):
        taps = []
        for tap in range(TAPS):
            start = LON_REACH + (tap - HALF) * dilation
            for group in range(GROUPS):
                piece = wide[group, row, pl.ds(start, cols), :]
                taps.append(piece.astype(jnp.bfloat16))
        totals.append(
            jnp.dot(
                jnp.concatenate(taps, 1), weight[...], preferred_element_type=jnp.float32
            )
        )
    return totals


def lon_first(split, info, *refs):
    pieces, states = refs[:5], refs[5:8]
    ocean, gain, weight, state_out = refs[8:12]
    normed, wide = refs[12:-1], refs[-1]
    totals = lon_total(info[3], pieces, weight, wide)
    values = []
    for row, total in enumerate(totals):
        total = total * ocean[0][:, row : row + 1]
        old = jnp.concatenate([ref[row] for ref in states], 0)
        new = (old.astype(jnp.float32) + total).astype(jnp.bfloat16)
        state_out[row] = new
        values.append(scaled(new.astype(jnp.float32), gain[...]).astype(jnp.bfloat16))

    def put(ref):
        for row, value in enumerate(values):
            ref[row] = value

    if split:
        first = pl.program_id(0) < pl.num_programs(0) // 2
        pl.when(first)(lambda: put(normed[0]))
        pl.when(jnp.logical_not(first))(lambda: put(normed[1]))
    else:
        put(normed[0])


def lon_mlp(info, base, left, middle, right, state, ocean, gain, weight, w_in, w_out, out, wide):
    totals = lon_total(info[4], (left, middle, right), weight, wide)
    for row, total in enumerate(totals):
        old = state[row].astype(jnp.float32)
        new = (old + total * ocean[0][:, row : row + 1]).astype(jnp.bfloat16).astype(jnp.float32)
        lifted = scaled(new, gain[...]).astype(jnp.bfloat16)
        half = 0.5 * jnp.dot(lifted, w_in[...], preferred_element_type=jnp.float32)
        hidden = (half + half * jnp.tanh(half)).astype(jnp.bfloat16)
        update = jnp.dot(hidden, w_out[...], preferred_element_type=jnp.float32)
        out[row] = (new + update).astype(jnp.bfloat16)


def whole(array):
    dims = array.ndim
    return pl.BlockSpec(array.shape, lambda *_: (0,) * dims, pipeline_mode=pl.Buffered(1))


def launch(body, scalars, grid, specs, out_specs, out_shape, scratch, flops, args):
    moved = sum(s.size * 2 for s in jax.tree.leaves(out_shape)) * 2
    return pl.pallas_call(
        body,
        grid_spec=pltpu.PrefetchScalarGridSpec(
            num_scalar_prefetch=len(scalars),
            grid=(grid,),
            in_specs=specs,
            out_specs=out_specs,
            scratch_shapes=scratch,
        ),
        out_shape=out_shape,
        compiler_params=pltpu.CompilerParams(vmem_limit_bytes=VMEM_LIMIT),
        cost_estimate=pl.CostEstimate(flops=flops, bytes_accessed=moved, transcendentals=0),
    )(*scalars, *args)


def after(x, *others):
    return lax.optimization_barrier((x, *others))[0]


def on_device(
    fields,
    mix_gain,
    lat_weight,
    lon_weight,
    mlp_gain,
    w_in,
    w_out,
    lat_dilation,
    lon_dilation,
    ocean,
):
    bf16 = jnp.bfloat16
    rows, cols = fields.shape[1:3]
    spare = rows - REACH
    count = lax.axis_size("lat")
    around = lax.axis_size("lon")
    member = lax.rem(lax.axis_index("lat"), 2).astype(jnp.int32)
    other = 1 - member
    swap_pairs = [(i, i ^ 1) for i in range(count)]
    south_pairs = [(i, i + 2) for i in range(count - 2)]
    north_pairs = [(i + 2, i) for i in range(count - 2)]
    near_pairs = [p for p in north_pairs if p[0] % 2 == 0] + [p for p in south_pairs if p[0] % 2]
    far_pairs = [p for p in south_pairs if p[0] % 2 == 0] + [p for p in north_pairs if p[0] % 2]
    east_pairs = [(i, (i + 1) % around) for i in range(around)]
    west_pairs = [((i + 1) % around, i) for i in range(around)]

    def swap(x):
        return lax.ppermute(x, "lat", swap_pairs)

    def lon_halo(head, tail):
        return lax.ppermute(tail, "lon", east_pairs), lax.ppermute(head, "lon", west_pairs)

    def lat_flops(r, c):
        return 2 * r * c * TAPS * C * C

    def cut(sample, at, size):
        return lax.dynamic_slice(fields, (sample, at, 0, 0), (1, size, cols, C))[0]

    edge = swap(cut(other, member * spare, REACH))
    rest = swap(cut(other, other * REACH, spare))
    near = lax.ppermute(cut(member, member * spare, REACH), "lat", near_pairs)

    info = jnp.concatenate([member[None], lat_dilation, lon_dilation])
    send_edge_base = jnp.stack([other * (REACH // TILE_ROWS)])
    keep_edge_base = jnp.stack([member * (REACH // TILE_ROWS)])
    lat_w = [block_diagonal(lat_weight[l]) for l in range(LAYERS)]
    lon_w = [block_diagonal(lon_weight[l]) for l in range(LAYERS)]
    gains = [mix_gain[0:1], mix_gain[1:2], mlp_gain[None]]

    early = (info, send_edge_base, keep_edge_base, *lat_w, *lon_w, *gains)
    edge, info, send_edge_base, keep_edge_base, w0, w1, v0, v1, *gains = lax.optimization_barrier(
        (edge, *early)
    )
    lat_w, lon_w = (w0, w1), (v0, v1)
    far = lax.ppermute(edge, "lat", far_pairs)

    wet = after(ocean, edge).astype(jnp.float32)
    wet_came = swap(wet)
    wet = jnp.where(
        member == 0, jnp.concatenate([wet, wet_came], 0), jnp.concatenate([wet_came, wet], 0)
    )
    tiles = 2 * rows // TILE_ROWS
    wet = wet.reshape(tiles, TILE_ROWS, cols).transpose(0, 2, 1)
    rest = after(rest, wet)
    edge_tiles = REACH // TILE_ROWS
    inner_tiles = tiles - 2 * edge_tiles

    def edge_tile(i):
        return jnp.where(i < edge_tiles, i, i + inner_tiles)

    def inner_tile(i):
        return i + edge_tiles

    strips = cols // TILE_COLS
    one = jax.ShapeDtypeStruct((2 * rows, TILE_COLS, C), bf16)

    def first_lat(grid, place, out_specs, out_shape, rest):
        strip = lambda size: pl.BlockSpec((size, TILE_COLS, C), lambda i, s: (0, place(i), 0))
        return launch(
            lat_first,
            (info,),
            grid,
            [
                pl.BlockSpec((1, rows, TILE_COLS, C), lambda i, s: (s[0], 0, place(i), 0)),
                strip(REACH),
                strip(spare),
                strip(REACH),
                strip(REACH),
                whole(gains[0]),
                whole(lat_w[0]),
            ],
            out_specs,
            out_shape,
            [pltpu.VMEM((2 * rows + 2 * REACH, TILE_COLS, C), bf16)],
            lat_flops(2 * rows, grid * TILE_COLS),
            (fields, edge, rest, near, far, gains[0], lat_w[0]),
        )

    fixed = pl.BlockSpec((2 * rows, TILE_COLS, C), lambda i, s: (0, 0, 0))
    head, tail, state_head, state_tail = first_lat(
        2, lambda i: i * (strips - 1), [fixed] * 4, [one] * 4, rest
    )
    left, right = lon_halo(head, tail)
    inside = (strips - 2) * TILE_COLS
    middle, state_middle = first_lat(
        strips - 2,
        lambda i: i + 1,
        [pl.BlockSpec((2 * rows, TILE_COLS, C), lambda i, s: (0, i, 0))] * 2,
        [jax.ShapeDtypeStruct((2 * rows, inside, C), bf16)] * 2,
        after(rest, head),
    )
    wide = pltpu.VMEM((GROUPS, TILE_ROWS, cols + 2 * LON_REACH, CG), jnp.float32)

    def first_pair(split, to_tile):
        number = 2 * edge_tiles if split else inner_tiles
        half = edge_tiles
        band = lambda width: pl.BlockSpec((TILE_ROWS, width, C), lambda i, s: (to_tile(i), 0, 0))
        shape = lambda n: jax.ShapeDtypeStruct((n * TILE_ROWS, cols, C), bf16)
        block = (TILE_ROWS, cols, C)
        specs = [pl.BlockSpec(block, lambda i, s: (i, 0, 0))]
        shapes = [shape(number)]
        if split:
            specs.append(pl.BlockSpec(block, lambda i, s: (jnp.minimum(i, half - 1), 0, 0)))
            specs.append(pl.BlockSpec(block, lambda i, s: (jnp.maximum(i - half, 0), 0, 0)))
            shapes += [shape(half)] * 2
        else:
            specs.append(specs[0])
            shapes.append(shape(number))
        widths = (TILE_COLS, inside, TILE_COLS)
        return launch(
            functools.partial(lon_first, split),
            (info,),
            number,
            [band(n) for n in (LON_REACH, *widths, LON_REACH, *widths)]
            + [
                pl.BlockSpec((1, cols, TILE_ROWS), lambda i, s: (to_tile(i), 0, 0)),
                whole(gains[1]),
                whole(lon_w[0]),
            ],
            specs,
            shapes,
            [wide],
            lat_flops(number * TILE_ROWS, cols),
            (
                left,
                head,
                middle,
                tail,
                right,
                state_head,
                state_middle,
                state_tail,
                wet,
                gains[1],
                lon_w[0],
            ),
        )

    edge_state, top, bottom = first_pair(True, edge_tile)
    north = lax.ppermute(bottom, "lat", south_pairs)
    south = lax.ppermute(top, "lat", north_pairs)
    inner_state, inner_normed = first_pair(False, inner_tile)

    inner_rows = inner_state.shape[0]
    strip = lambda size: pl.BlockSpec((size, TILE_COLS, C), lambda i, s: (0, i, 0))

    def second_lat(body, out_rows, held_rows, args):
        end = pl.BlockSpec((out_rows, TILE_COLS, C), lambda i, s: (0, 0, 0))
        end_shape = jax.ShapeDtypeStruct((out_rows, TILE_COLS, C), bf16)
        return launch(
            body,
            (info,),
            strips,
            [strip(a.shape[0]) for a in args] + [whole(lat_w[1])],
            [strip(out_rows), end, end],
            [jax.ShapeDtypeStruct((out_rows, cols, C), bf16), end_shape, end_shape],
            [pltpu.VMEM((held_rows, TILE_COLS, C), bf16)],
            lat_flops(out_rows, cols),
            (*args, lat_w[1]),
        )

    inner_across, head, tail = second_lat(
        lat_inner, inner_rows, 2 * REACH + inner_rows, (top, bottom, inner_normed)
    )
    inner_halo = lon_halo(head, tail)

    def second(acr, halo, old, to_tile, base, number):
        band = lambda width: pl.BlockSpec((TILE_ROWS, width, C), lambda i, s, b: (b[0] + i, 0, 0))
        size = number * TILE_ROWS
        return launch(
            lon_mlp,
            (info, base),
            number,
            [
                band(LON_REACH),
                band(cols),
                band(LON_REACH),
                band(cols),
                pl.BlockSpec((1, cols, TILE_ROWS), lambda i, s, b: (to_tile(b[0] + i), 0, 0)),
                whole(gains[2]),
                whole(lon_w[1]),
                whole(w_in),
                whole(w_out),
            ],
            pl.BlockSpec((TILE_ROWS, cols, C), lambda i, s, b: (i, 0, 0)),
            jax.ShapeDtypeStruct((size, cols, C), bf16),
            [wide],
            lat_flops(size, cols) + 16 * size * cols * C * C,
            (halo[0], acr, halo[1], old, wet, gains[2], lon_w[1], w_in, w_out),
        )

    half_inner = inner_tiles // 2
    send_inner = second(
        inner_across, inner_halo, inner_state, inner_tile, send_edge_base, half_inner
    )
    back_inner = swap(send_inner)
    north = after(north, send_inner)
    edge_across, head, tail = second_lat(
        lat_edge, 2 * REACH, 4 * REACH + inner_rows, (top, bottom, inner_normed, north, south)
    )
    edge_halo = lon_halo(head, tail)
    send_edge = second(edge_across, edge_halo, edge_state, edge_tile, send_edge_base, edge_tiles)
    back_edge = swap(send_edge)
    keep_inner = second(
        after(inner_across, send_edge),
        inner_halo,
        inner_state,
        inner_tile,
        keep_edge_base,
        half_inner,
    )
    keep_edge = second(
        after(edge_across, send_edge), edge_halo, edge_state, edge_tile, keep_edge_base, edge_tiles
    )
    out = jnp.zeros(fields.shape, bf16)
    edge_at = member * spare
    inner_at = other * REACH
    for piece, sample, at in (
        (keep_inner, member, inner_at),
        (keep_edge, member, edge_at),
        (back_inner, other, inner_at),
        (back_edge, other, edge_at),
    ):
        out = lax.dynamic_update_slice(out, piece[None], (sample, at, 0, 0))
    return out


def solution(mesh):
    return jax.shard_map(
        on_device,
        mesh=mesh,
        in_specs=(
            P("grp", "lat", "lon", None),
            P(),
            P(),
            P(),
            P(),
            P(),
            P(),
            P(),
            P(),
            P(("grp", "lat"), "lon"),
        ),
        out_specs=P("grp", "lat", "lon", None),
        check_vma=False,
    )
```

profile of v0, /device:TPU:0, one launch (start us, length us, event | category | flops | bytes accessed | tf_op | source)
XLA Modules:
  0.0 132.8 jit_solution(5218744841174227957)
XLA Ops:
  0.0 3.1 %dynamic-slice_bitcast_fusion = (bf16[8,192,256]{2,1,0:T(8,128)(2,1)}, bf16[8,192,256]{2,1,0:T(8,128)(2,1)}, bf16[8,192,256]{2,1,0:T(8,128)(2,1)}) fusion(bf16[2,16,192,256]{3,2,1,0:T(8,128)(2,1)} %own.3, s32[]{:T(128)S(6)} %select_n.40, s32[]{:T(128)S(6)} %select_n.35, s32[]{:T(128)S(6)} %select_n.34, s32[]{:T(128)S(6)} %select_n.36), kind=kLoop, calls=%fused_computation.14 | loop fusion | bytes 4718608 | tf_op jit(solution)/shard_map/squeeze | solution.py:244
  3.1 3.0 %collective-permute-start = (bf16[8,192,256]{2,1,0:T(8,128)(2,1)}, bf16[8,192,256]{2,1,0:T(8,128)(2,1)S(1)}, u32[]{:S(2)}, u32[]{:S(2)}) collective-permute-start(bf16[8,192,256]{2,1,0:T(8,128)(2,1)} %get-tuple-element.75), channel_id=1, source_target_pairs={{0,2},{2,0},{4,6},{6,4},{8,10},{10,8},{12,14},{14,12},{1,3},{3,1},... | collective-permute-start | bytes 2359304 | tf_op jit(solution)/shard_map/ppermute | solution.py:235
  6.1 1.3 collective-permute-start.3
  7.6 0.8 slice_bitcast_fusion.9
  8.8 0.7 copy-done.13
  9.6 15.1 %collective-permute-done.edge = bf16[8,192,256]{2,1,0:T(8,128)(2,1)S(1)} collective-permute-done((bf16[8,192,256]{2,1,0:T(8,128)(2,1)}, bf16[8,192,256]{2,1,0:T(8,128)(2,1)S(1)}, u32[]{:S(2)}, u32[]{:S(2)}) %collective-permute-start) | collective-permute-done | bytes 786464 | tf_op jit(solution)/shard_map/ppermute | solution.py:235
  24.7 4.9 %collective-permute-start.4 = (bf16[8,192,256]{2,1,0:T(8,128)(2,1)S(1)}, bf16[8,192,256]{2,1,0:T(8,128)(2,1)}, u32[]{:S(2)}, u32[]{:S(2)}) collective-permute-start(bf16[8,192,256]{2,1,0:T(8,128)(2,1)S(1)} %collective-permute-done.edge), channel_id=1, source_target_pairs={{0,4},{4,8},{8,12},{6,2},{10,6},{14,10},{1,5},{5,9},{9,13},{7,3},{... | collective-permute-start | bytes 2359304 | tf_op jit(solution)/shard_map/ppermute | solution.py:262
  29.6 11.4 %collective-permute-done.2 = f32[16,192]{1,0:T(8,128)S(1)} collective-permute-done((f32[16,192]{1,0:T(8,128)S(1)}, f32[16,192]{1,0:T(8,128)S(1)}, u32[]{:S(2)}, u32[]{:S(2)}) %collective-permute-start.2) | collective-permute-done | bytes 12320 | tf_op jit(solution)/shard_map/ppermute | solution.py:235
  41.1 1.2 copy.19
  42.3 1.3 collective-permute-done.4.far
  43.6 5.2 %shard_map.100 = (bf16[32,48,256]{2,1,0:T(8,128)(2,1)S(1)}, bf16[32,48,256]{2,1,0:T(8,128)(2,1)S(1)}, bf16[32,48,256]{2,1,0:T(8,128)(2,1)S(1)}, bf16[32,48,256]{2,1,0:T(8,128)(2,1)S(1)}) custom-call(s32[5]{0:T(128)S(1)} %pad_add_fusion.info, bf16[2,16,192,256]{3,2,1,0:T(8,128)(2,1)} %own.3, bf16[8,192,256]{2,1,0:T(8,128)(2,1)S(1)} %collective-permute-done.edge, ...), custom_call_target="tpu_custom_call" | custom-call | flops 2013265920 | bytes 6291456 | tf_op jit(solution)/shard_map/pallas_call | solution.py:188
  48.8 0.5 collective-permute-start.6
  49.3 6.1 %shard_map.101 = (bf16[32,96,256]{2,1,0:T(8,128)(2,1)S(1)}, bf16[32,96,256]{2,1,0:T(8,128)(2,1)}) custom-call(s32[5]{0:T(128)S(1)} %pad_add_fusion.info, bf16[2,16,192,256]{3,2,1,0:T(8,128)(2,1)} %own.3, bf16[8,192,256]{2,1,0:T(8,128)(2,1)S(1)} %collective-permute-done.edge, bf16[8,192,256]{2,1,0:T(8,128)(2,1)} %collective-permute-done.1.rest, ...), custom_call_target="tpu_custom_call" | custom-call | flops 2013265920 | bytes 6291456 | tf_op jit(solution)/shard_map/pallas_call | solution.py:188
  55.5 1.2 copy-done.1
  56.7 6.9 %shard_map.102 = (bf16[16,192,256]{2,1,0:T(8,128)(2,1)}, bf16[8,192,256]{2,1,0:T(8,128)(2,1)S(1)}, bf16[8,192,256]{2,1,0:T(8,128)(2,1)S(1)}) custom-call(s32[5]{0:T(128)S(1)} %pad_add_fusion.info, bf16[32,48,256]{2,1,0:T(8,128)(2,1)S(1)} %collective-permute-done.5.refs_0_, bf16[32,48,256]{2,1,0:T(8,128)(2,1)S(1)} %get-tuple-element.47.refs_1_, ...), custom_call_target="tpu_custom_call" | custom-call | flops 2013265920 | bytes 6291456 | tf_op jit(solution)/shard_map/pallas_call | solution.py:188
  63.5 4.5 %collective-permute-start.8 = (bf16[8,192,256]{2,1,0:T(8,128)(2,1)S(1)}, bf16[8,192,256]{2,1,0:T(8,128)(2,1)S(1)}, u32[]{:S(2)}, u32[]{:S(2)}) collective-permute-start(bf16[8,192,256]{2,1,0:T(8,128)(2,1)S(1)} %get-tuple-element.56.bottom), channel_id=1, source_target_pairs={{0,4},{2,6},{4,8},{6,10},{8,12},{10,14},{1,5},{3,7},{5,9},{7,11},{... | collective-permute-start | bytes 2359304 | tf_op jit(solution)/shard_map/ppermute | solution.py:367
  68.1 1.5 %collective-permute-start.10 = (bf16[8,192,256]{2,1,0:T(8,128)(2,1)S(1)}, bf16[8,192,256]{2,1,0:T(8,128)(2,1)}, u32[]{:S(2)}, u32[]{:S(2)}) collective-permute-start(bf16[8,192,256]{2,1,0:T(8,128)(2,1)S(1)} %get-tuple-element.55.top), channel_id=1, source_target_pairs={{4,0},{6,2},{8,4},{10,6},{12,8},{14,10},{5,1},{7,3},{9,5},{11,7},{... | collective-permute-start | bytes 2359304 | tf_op jit(solution)/shard_map/ppermute | solution.py:368
  69.6 6.7 %shard_map.103 = (bf16[16,192,256]{2,1,0:T(8,128)(2,1)}, bf16[16,192,256]{2,1,0:T(8,128)(2,1)}) custom-call(s32[5]{0:T(128)S(1)} %pad_add_fusion.info, bf16[32,48,256]{2,1,0:T(8,128)(2,1)S(1)} %collective-permute-done.5.refs_0_, bf16[32,48,256]{2,1,0:T(8,128)(2,1)S(1)} %get-tuple-element.47.refs_1_, bf16[32,96,256]{2,1,0:T(8,128)(2,1)} %copy-done.1, ...), custom_call_target="tpu_custom_call" | custom-call | flops 2013265920 | bytes 6291456 | tf_op jit(solution)/shard_map/pallas_call | solution.py:188
  76.2 1.4 %copy-done.4 = bf16[16,192,256]{2,1,0:T(8,128)(2,1)S(1)} copy-done((bf16[16,192,256]{2,1,0:T(8,128)(2,1)S(1)}, bf16[16,192,256]{2,1,0:T(8,128)(2,1)}, u32[]{:S(2)}) %copy-start.4) | copy-done | bytes 1572888
  77.6 3.8 %shard_map.104 = (bf16[16,192,256]{2,1,0:T(8,128)(2,1)S(1)}, bf16[16,48,256]{2,1,0:T(8,128)(2,1)S(1)}, bf16[16,48,256]{2,1,0:T(8,128)(2,1)S(1)}) custom-call(s32[5]{0:T(128)S(1)} %pad_add_fusion.info, bf16[8,192,256]{2,1,0:T(8,128)(2,1)S(1)} %get-tuple-element.55.top, bf16[8,192,256]{2,1,0:T(8,128)(2,1)S(1)} %get-tuple-element.56.bottom, ...), custom_call_target="tpu_custom_call" | custom-call | flops 2013265920 | bytes 4718592 | tf_op jit(solution)/shard_map/pallas_call | solution.py:188
  81.5 0.5 collective-permute-start.9
  82.0 1.2 collective-permute-done.7.left
  83.2 0.6 collective-permute-done.9.right
  83.8 5.8 %shard_map.105 = bf16[8,192,256]{2,1,0:T(8,128)(2,1)S(1)} custom-call(s32[5]{0:T(128)S(1)} %pad_add_fusion.info, s32[1]{0:T(128)} %bitcast.2.base, bf16[16,48,256]{2,1,0:T(8,128)(2,1)S(1)} %collective-permute-done.7.left, bf16[16,192,256]{2,1,0:T(8,128)(2,1)S(1)} %get-tuple-element.71.middle, bf16[16,48,256]{2,1,0:T(8,128)(2,1)S(1)} %collective-permute-done.9.right, ...), custom_call_target="tpu_custom_call" | custom-call | flops 2617245696 | bytes 1572864 | tf_op jit(solution)/shard_map/pallas_call | solution.py:188
  89.7 5.2 %shard_map.106 = (bf16[16,192,256]{2,1,0:T(8,128)(2,1)S(1)}, bf16[16,48,256]{2,1,0:T(8,128)(2,1)S(1)}, bf16[16,48,256]{2,1,0:T(8,128)(2,1)S(1)}) custom-call(s32[5]{0:T(128)S(1)} %pad_add_fusion.info, bf16[8,192,256]{2,1,0:T(8,128)(2,1)S(1)} %get-tuple-element.55.top, bf16[8,192,256]{2,1,0:T(8,128)(2,1)S(1)} %get-tuple-element.56.bottom, ...), custom_call_target="tpu_custom_call" | custom-call | flops 2013265920 | bytes 4718592 | tf_op jit(solution)/shard_map/pallas_call | solution.py:188
  95.5 1.5 %collective-permute-start.13 = (bf16[8,192,256]{2,1,0:T(8,128)(2,1)S(1)}, bf16[8,192,256]{2,1,0:T(8,128)(2,1)S(1)}, u32[]{:S(2)}, u32[]{:S(2)}) collective-permute-start(bf16[8,192,256]{2,1,0:T(8,128)(2,1)S(1)} %shard_map.105), channel_id=1, source_target_pairs={{0,2},{2,0},{4,6},{6,4},{8,10},{10,8},{12,14},{14,12},{1,3},{3,1},... | collective-permute-start | bytes 2359304 | tf_op jit(solution)/shard_map/ppermute | solution.py:235
  97.2 5.8 %shard_map.107 = bf16[8,192,256]{2,1,0:T(8,128)(2,1)S(1)} custom-call(s32[5]{0:T(128)S(1)} %pad_add_fusion.info, s32[1]{0:T(128)} %bitcast.2.base, bf16[16,48,256]{2,1,0:T(8,128)(2,1)S(1)} %collective-permute-done.11.left, bf16[16,192,256]{2,1,0:T(8,128)(2,1)S(1)} %get-tuple-element.72.middle, bf16[16,48,256]{2,1,0:T(8,128)(2,1)S(1)} %collective-permute-done.12.right, ...), custom_call_target="tpu_custom_call" | custom-call | flops 2617245696 | bytes 1572864 | tf_op jit(solution)/shard_map/pallas_call | solution.py:188
  103.1 1.6 %collective-permute-start.14 = (bf16[8,192,256]{2,1,0:T(8,128)(2,1)S(1)}, bf16[8,192,256]{2,1,0:T(8,128)(2,1)S(1)}, u32[]{:S(2)}, u32[]{:S(2)}) collective-permute-start(bf16[8,192,256]{2,1,0:T(8,128)(2,1)S(1)} %shard_map.107), channel_id=1, source_target_pairs={{0,2},{2,0},{4,6},{6,4},{8,10},{10,8},{12,14},{14,12},{1,3},{3,1},... | collective-permute-start | bytes 2359304 | tf_op jit(solution)/shard_map/ppermute | solution.py:235
  104.7 5.8 %shard_map.109 = bf16[8,192,256]{2,1,0:T(8,128)(2,1)S(1)} custom-call(s32[5]{0:T(128)S(1)} %pad_add_fusion.info, s32[1]{0:T(128)} %bitcast.3.base, bf16[16,48,256]{2,1,0:T(8,128)(2,1)S(1)} %collective-permute-done.11.left, bf16[16,192,256]{2,1,0:T(8,128)(2,1)S(1)} %get-tuple-element.72.middle, bf16[16,48,256]{2,1,0:T(8,128)(2,1)S(1)} %collective-permute-done.12.right, ...), custom_call_target="tpu_custom_call" | custom-call | flops 2617245696 | bytes 1572864 | tf_op jit(solution)/shard_map/pallas_call | solution.py:188
  110.5 5.8 %shard_map.108 = bf16[8,192,256]{2,1,0:T(8,128)(2,1)S(1)} custom-call(s32[5]{0:T(128)S(1)} %pad_add_fusion.info, s32[1]{0:T(128)} %bitcast.3.base, bf16[16,48,256]{2,1,0:T(8,128)(2,1)S(1)} %collective-permute-done.7.left, bf16[16,192,256]{2,1,0:T(8,128)(2,1)S(1)} %copy-done.9, bf16[16,48,256]{2,1,0:T(8,128)(2,1)S(1)} %collective-permute-done.9.right, ...), custom_call_target="tpu_custom_call" | custom-call | flops 2617245696 | bytes 1572864 | tf_op jit(solution)/shard_map/pallas_call | solution.py:188
  116.9 14.9 %collective-permute-done.14 = bf16[8,192,256]{2,1,0:T(8,128)(2,1)S(1)} collective-permute-done((bf16[8,192,256]{2,1,0:T(8,128)(2,1)S(1)}, bf16[8,192,256]{2,1,0:T(8,128)(2,1)S(1)}, u32[]{:S(2)}, u32[]{:S(2)}) %collective-permute-start.14) | collective-permute-done | bytes 786464 | tf_op jit(solution)/shard_map/ppermute | solution.py:235
  131.9 0.9 bitcast_dynamic-update-slice_fusion
  (66 shorter events, 2.2 us)
Async XLA Ops:
  0.0 7.4 %copy-start.11 = (bf16[2,5,2,128,128]{4,3,2,1,0:T(8,128)(2,1)S(1)}, bf16[2,5,2,128,128]{4,3,2,1,0:T(8,128)(2,1)}, u32[]{:S(2)}) copy-start(bf16[2,5,2,128,128]{4,3,2,1,0:T(8,128)(2,1)} %param.12) | copy-start | bytes 1966084
  3.1 4.4 %copy-start.12 = (bf16[2,5,2,128,128]{4,3,2,1,0:T(8,128)(2,1)S(1)}, bf16[2,5,2,128,128]{4,3,2,1,0:T(8,128)(2,1)}, u32[]{:S(2)}) copy-start(bf16[2,5,2,128,128]{4,3,2,1,0:T(8,128)(2,1)} %param.13) | copy-start | bytes 1966084
  3.1 21.5 %collective-permute-start = (bf16[8,192,256]{2,1,0:T(8,128)(2,1)}, bf16[8,192,256]{2,1,0:T(8,128)(2,1)S(1)}, u32[]{:S(2)}, u32[]{:S(2)}) collective-permute-start(bf16[8,192,256]{2,1,0:T(8,128)(2,1)} %get-tuple-element.75), channel_id=1, source_target_pairs={{0,2},{2,0},{4,6},{6,4},{8,10},{10,8},{12,14},{14,12},{1,3},{3,1},... | collective-permute-start | bytes 2359304 | tf_op jit(solution)/shard_map/ppermute | solution.py:235
  6.1 36.2 %collective-permute-start.1 = (bf16[8,192,256]{2,1,0:T(8,128)(2,1)}, bf16[8,192,256]{2,1,0:T(8,128)(2,1)}, u32[]{:S(2)}, u32[]{:S(2)}) collective-permute-start(bf16[8,192,256]{2,1,0:T(8,128)(2,1)} %get-tuple-element.74), channel_id=1, source_target_pairs={{0,2},{2,0},{4,6},{6,4},{8,10},{10,8},{12,14},{14,12},{1,3},{3,1},... | collective-permute-start | bytes 2359304 | tf_op jit(solution)/shard_map/ppermute | solution.py:235
  6.1 36.1 %collective-permute-start.3 = (bf16[8,192,256]{2,1,0:T(8,128)(2,1)}, bf16[8,192,256]{2,1,0:T(8,128)(2,1)}, u32[]{:S(2)}, u32[]{:S(2)}) collective-permute-start(bf16[8,192,256]{2,1,0:T(8,128)(2,1)} %get-tuple-element.73), channel_id=1, source_target_pairs={{4,0},{8,4},{12,8},{2,6},{6,10},{10,14},{5,1},{9,5},{13,9},{3,7},{... | collective-permute-start | bytes 2359304 | tf_op jit(solution)/shard_map/ppermute | solution.py:248
  8.5 0.9 copy-start.13
  8.5 1.0 copy-start.14
  8.6 1.0 copy-start.16
  8.6 21.0 %copy-start.15 = (s32[16,192]{1,0:T(8,128)S(1)}, s32[16,192]{1,0:T(8,128)}, u32[]{:S(2)}) copy-start(s32[16,192]{1,0:T(8,128)} %param.19) | copy-start | bytes 36868
  24.7 18.9 %collective-permute-start.4 = (bf16[8,192,256]{2,1,0:T(8,128)(2,1)S(1)}, bf16[8,192,256]{2,1,0:T(8,128)(2,1)}, u32[]{:S(2)}, u32[]{:S(2)}) collective-permute-start(bf16[8,192,256]{2,1,0:T(8,128)(2,1)S(1)} %collective-permute-done.edge), channel_id=1, source_target_pairs={{0,4},{4,8},{8,12},{6,2},{10,6},{14,10},{1,5},{5,9},{9,13},{7,3},{... | collective-permute-start | bytes 2359304 | tf_op jit(solution)/shard_map/ppermute | solution.py:262
  29.6 11.5 %collective-permute-start.2 = (f32[16,192]{1,0:T(8,128)S(1)}, f32[16,192]{1,0:T(8,128)S(1)}, u32[]{:S(2)}, u32[]{:S(2)}) collective-permute-start(f32[16,192]{1,0:T(8,128)S(1)} %convert_element_type.3), channel_id=1, source_target_pairs={{0,2},{2,0},{4,6},{6,4},{8,10},{10,8},{12,14},{14,12},{1,3},{3,1},... | collective-permute-start | bytes 36872 | tf_op jit(solution)/shard_map/ppermute | solution.py:235
  48.7 6.7 %copy-start.2 = (bf16[32,48,256]{2,1,0:T(8,128)(2,1)}, bf16[32,48,256]{2,1,0:T(8,128)(2,1)S(1)}, u32[]{:S(2)}) copy-start(bf16[32,48,256]{2,1,0:T(8,128)(2,1)S(1)} %get-tuple-element.52.refs_7_) | copy-start | bytes 2359300
  48.8 7.9 %collective-permute-start.5 = (bf16[32,48,256]{2,1,0:T(8,128)(2,1)S(1)}, bf16[32,48,256]{2,1,0:T(8,128)(2,1)S(1)}, u32[]{:S(2)}, u32[]{:S(2)}) collective-permute-start(bf16[32,48,256]{2,1,0:T(8,128)(2,1)S(1)} %get-tuple-element.46.refs_3_), channel_id=1, source_target_pairs={{0,1},{1,0},{2,3},{3,2},{4,5},{5,4},{6,7},{7,6},{8,9},{9,8},{10,11... | collective-permute-start | bytes 2359304 | tf_op jit(solution)/shard_map/ppermute | solution.py:238
  48.8 7.8 %collective-permute-start.6 = (bf16[32,48,256]{2,1,0:T(8,128)(2,1)S(1)}, bf16[32,48,256]{2,1,0:T(8,128)(2,1)S(1)}, u32[]{:S(2)}, u32[]{:S(2)}) collective-permute-start(bf16[32,48,256]{2,1,0:T(8,128)(2,1)S(1)} %get-tuple-element.47.refs_1_), channel_id=1, source_target_pairs={{1,0},{0,1},{3,2},{2,3},{5,4},{4,5},{7,6},{6,7},{9,8},{8,9},{11,10... | collective-permute-start | bytes 2359304 | tf_op jit(solution)/shard_map/ppermute | solution.py:238
  55.5 1.2 copy-start.1
  56.6 12.9 %copy-start = (f32[8,4,192]{1,2,0:T(8,128)S(1)}, f32[8,4,192]{1,2,0:T(8,128)}, u32[]{:S(2)}) copy-start(f32[8,4,192]{1,2,0:T(8,128)} %copy.19) | copy-start | bytes 73732
  56.6 12.9 %copy-start.3 = (bf16[32,48,256]{2,1,0:T(8,128)(2,1)S(1)}, bf16[32,48,256]{2,1,0:T(8,128)(2,1)}, u32[]{:S(2)}) copy-start(bf16[32,48,256]{2,1,0:T(8,128)(2,1)} %copy-done.2) | copy-start | bytes 2359300
  63.5 26.2 %collective-permute-start.8 = (bf16[8,192,256]{2,1,0:T(8,128)(2,1)S(1)}, bf16[8,192,256]{2,1,0:T(8,128)(2,1)S(1)}, u32[]{:S(2)}, u32[]{:S(2)}) collective-permute-start(bf16[8,192,256]{2,1,0:T(8,128)(2,1)S(1)} %get-tuple-element.56.bottom), channel_id=1, source_target_pairs={{0,4},{2,6},{4,8},{6,10},{8,12},{10,14},{1,5},{3,7},{5,9},{7,11},{... | collective-permute-start | bytes 2359304 | tf_op jit(solution)/shard_map/ppermute | solution.py:367
  68.1 21.6 %collective-permute-start.10 = (bf16[8,192,256]{2,1,0:T(8,128)(2,1)S(1)}, bf16[8,192,256]{2,1,0:T(8,128)(2,1)}, u32[]{:S(2)}, u32[]{:S(2)}) collective-permute-start(bf16[8,192,256]{2,1,0:T(8,128)(2,1)S(1)} %get-tuple-element.55.top), channel_id=1, source_target_pairs={{4,0},{6,2},{8,4},{10,6},{12,8},{14,10},{5,1},{7,3},{9,5},{11,7},{... | collective-permute-start | bytes 2359304 | tf_op jit(solution)/shard_map/ppermute | solution.py:368
  76.2 1.4 %copy-start.4 = (bf16[16,192,256]{2,1,0:T(8,128)(2,1)S(1)}, bf16[16,192,256]{2,1,0:T(8,128)(2,1)}, u32[]{:S(2)}) copy-start(bf16[16,192,256]{2,1,0:T(8,128)(2,1)} %get-tuple-element.57.inner) | copy-start | bytes 4718596
  77.6 6.2 %copy-start.5 = (bf16[256,1024]{1,0:T(8,128)(2,1)S(1)}, bf16[256,1024]{1,0:T(8,128)(2,1)}, u32[]{:S(2)}) copy-start(bf16[256,1024]{1,0:T(8,128)(2,1)} %w_in.7) | copy-start | bytes 1572868
  77.6 6.2 %copy-start.6 = (bf16[1024,256]{1,0:T(8,128)(2,1)S(1)}, bf16[1024,256]{1,0:T(8,128)(2,1)}, u32[]{:S(2)}) copy-start(bf16[1024,256]{1,0:T(8,128)(2,1)} %w_out.7) | copy-start | bytes 1572868
  77.6 6.2 %copy-start.7 = (f32[256]{0:T(256)S(1)}, f32[256]{0:T(256)}, u32[]{:S(2)}) copy-start(f32[256]{0:T(256)} %param.14) | copy-start | bytes 3076
  81.4 8.2 %copy-start.8 = (bf16[16,192,256]{2,1,0:T(8,128)(2,1)}, bf16[16,192,256]{2,1,0:T(8,128)(2,1)S(1)}, u32[]{:S(2)}) copy-start(bf16[16,192,256]{2,1,0:T(8,128)(2,1)S(1)} %get-tuple-element.71.middle) | copy-start | bytes 4718596
  81.5 1.8 %collective-permute-start.7 = (bf16[16,48,256]{2,1,0:T(8,128)(2,1)S(1)}, bf16[16,48,256]{2,1,0:T(8,128)(2,1)S(1)}, u32[]{:S(2)}, u32[]{:S(2)}) collective-permute-start(bf16[16,48,256]{2,1,0:T(8,128)(2,1)S(1)} %get-tuple-element.59), channel_id=1, source_target_pairs={{0,1},{1,0},{2,3},{3,2},{4,5},{5,4},{6,7},{7,6},{8,9},{9,8},{10,11... | collective-permute-start | bytes 1179656 | tf_op jit(solution)/shard_map/ppermute | solution.py:238
  81.5 2.3 %collective-permute-start.9 = (bf16[16,48,256]{2,1,0:T(8,128)(2,1)S(1)}, bf16[16,48,256]{2,1,0:T(8,128)(2,1)S(1)}, u32[]{:S(2)}, u32[]{:S(2)}) collective-permute-start(bf16[16,48,256]{2,1,0:T(8,128)(2,1)S(1)} %get-tuple-element.62), channel_id=1, source_target_pairs={{1,0},{0,1},{3,2},{2,3},{5,4},{4,5},{7,6},{6,7},{9,8},{8,9},{11,10... | collective-permute-start | bytes 1179656 | tf_op jit(solution)/shard_map/ppermute | solution.py:238
  94.9 2.1 %collective-permute-start.11 = (bf16[16,48,256]{2,1,0:T(8,128)(2,1)S(1)}, bf16[16,48,256]{2,1,0:T(8,128)(2,1)S(1)}, u32[]{:S(2)}, u32[]{:S(2)}) collective-permute-start(bf16[16,48,256]{2,1,0:T(8,128)(2,1)S(1)} %get-tuple-element.67), channel_id=1, source_target_pairs={{0,1},{1,0},{2,3},{3,2},{4,5},{5,4},{6,7},{7,6},{8,9},{9,8},{10,11... | collective-permute-start | bytes 1179656 | tf_op jit(solution)/shard_map/ppermute | solution.py:238
  95.1 2.2 %collective-permute-start.12 = (bf16[16,48,256]{2,1,0:T(8,128)(2,1)S(1)}, bf16[16,48,256]{2,1,0:T(8,128)(2,1)S(1)}, u32[]{:S(2)}, u32[]{:S(2)}) collective-permute-start(bf16[16,48,256]{2,1,0:T(8,128)(2,1)S(1)} %get-tuple-element.69), channel_id=1, source_target_pairs={{1,0},{0,1},{3,2},{2,3},{5,4},{4,5},{7,6},{6,7},{9,8},{8,9},{11,10... | collective-permute-start | bytes 1179656 | tf_op jit(solution)/shard_map/ppermute | solution.py:238
  95.5 21.4 %collective-permute-start.13 = (bf16[8,192,256]{2,1,0:T(8,128)(2,1)S(1)}, bf16[8,192,256]{2,1,0:T(8,128)(2,1)S(1)}, u32[]{:S(2)}, u32[]{:S(2)}) collective-permute-start(bf16[8,192,256]{2,1,0:T(8,128)(2,1)S(1)} %shard_map.105), channel_id=1, source_target_pairs={{0,2},{2,0},{4,6},{6,4},{8,10},{10,8},{12,14},{14,12},{1,3},{3,1},... | collective-permute-start | bytes 2359304 | tf_op jit(solution)/shard_map/ppermute | solution.py:235
  103.1 7.4 %copy-start.9 = (bf16[16,192,256]{2,1,0:T(8,128)(2,1)S(1)}, bf16[16,192,256]{2,1,0:T(8,128)(2,1)}, u32[]{:S(2)}) copy-start(bf16[16,192,256]{2,1,0:T(8,128)(2,1)} %copy-done.8) | copy-start | bytes 4718596
  103.1 28.8 %collective-permute-start.14 = (bf16[8,192,256]{2,1,0:T(8,128)(2,1)S(1)}, bf16[8,192,256]{2,1,0:T(8,128)(2,1)S(1)}, u32[]{:S(2)}, u32[]{:S(2)}) collective-permute-start(bf16[8,192,256]{2,1,0:T(8,128)(2,1)S(1)} %shard_map.107), channel_id=1, source_target_pairs={{0,2},{2,0},{4,6},{6,4},{8,10},{10,8},{12,14},{14,12},{1,3},{3,1},... | collective-permute-start | bytes 2359304 | tf_op jit(solution)/shard_map/ppermute | solution.py:235
  116.9 15.0 %copy-start.10 = (bf16[2,16,192,256]{3,2,1,0:T(8,128)(2,1)}, bf16[2,16,192,256]{3,2,1,0:T(8,128)(2,1)S(1)}, u32[]{:S(2)}) copy-start(bf16[2,16,192,256]{3,2,1,0:T(8,128)(2,1)S(1)} %bitcast_dynamic-update-slice_fusion.1) | copy-start | bytes 9437188
  (2 other events, 1.7 us)
where the time goes:
time: 134 us; the launch traced here: 133 us
  Pallas kernels  57.1 us (43%)
  waiting for transfers between devices  44.8 us (33%)
  starting transfers between devices  20 us (15%)
  local copies, waits for them, and re-layouts  10.2 us (8%)
    pallas_call x10, Pallas kernels, launch(): pl.pallas_call(body, grid_spec=pltpu.PrefetchScalarGridSpec(num_scalar_pr...  57.1 us
    ppermute x5, waiting for transfers between devices, swap(): return lax.ppermute(x, 'lat', swap_pairs)  41.5 us
    ppermute x5, starting transfers between devices, swap(): return lax.ppermute(x, 'lat', swap_pairs)  6.09 us
    ppermute x1, starting transfers between devices, on_device(): far = lax.ppermute(edge, 'lat', far_pairs)  4.91 us
    ppermute x1, starting transfers between devices, on_device(): north = lax.ppermute(bottom, 'lat', south_pairs)  4.54 us
    unnamed x38, local copies, waits for them, and re-layouts  3.42 us
    squeeze x1, local copies, waits for them, and re-layouts, cut(): return lax.dynamic_slice(fields, (sample, at, 0, 0), (1, size, cols, C))[0]  3.13 us
  transfers between devices with their start and end apart: 15, of which 7 were waited for; matrix products, arithmetic and copies ran while one was open for 2% of the time, Pallas kernels for 30%

commit v1 on v0

--- a/solution.py
+++ b/solution.py
@@ -19,6 +19,7 @@
 LON_REACH = HALF * MAXDIL_LON
 TILE_COLS = LON_REACH
 TILE_ROWS = 4
+COST_SHARE = 100000000
 VMEM_LIMIT = 48 * 1024 * 1024
 
 
@@ -100,18 +101,21 @@
     held[0:REACH] = top[...]
     held[REACH : REACH + rows] = inner[...]
     held[REACH + rows : 2 * REACH + rows] = bottom[...]
-    across[...] = conv_rows(held, weight, info[2], REACH, rows)
+    first = REACH + (1 - info[0]) * across.shape[0]
+    across[...] = conv_rows(held, weight, info[2], first, across.shape[0])
     put_ends(across, head, tail)
 
 
-def lat_edge(info, top, bottom, inner, north, south, weight, across, head, tail, held):
+def lat_others(info, top, bottom, inner, north, south, weight, across, head, tail, held):
     rows = inner.shape[0]
     at = 0
     for ref in (north, top, inner, bottom, south):
         held[at : at + ref.shape[0]] = ref[...]
         at += ref.shape[0]
+    half = rows // 2
     across[0:REACH] = conv_rows(held, weight, info[2], REACH, REACH)
-    across[REACH:] = conv_rows(held, weight, info[2], 2 * REACH + rows, REACH)
+    across[REACH : 2 * REACH] = conv_rows(held, weight, info[2], 2 * REACH + rows, REACH)
+    across[2 * REACH :] = conv_rows(held, weight, info[2], 2 * REACH + info[0] * half, half)
     put_ends(across, head, tail)
 
 
@@ -125,20 +129,16 @@
             ].astype(jnp.float32)
         at += width
     cols = at - 2 * LON_REACH
-    totals = []
-    for row in range(TILE_ROWS):
-        taps = []
-        for tap in range(TAPS):
-            start = LON_REACH + (tap - HALF) * dilation
-            for group in range(GROUPS):
-                piece = wide[group, row, pl.ds(start, cols), :]
-                taps.append(piece.astype(jnp.bfloat16))
-        totals.append(
-            jnp.dot(
-                jnp.concatenate(taps, 1), weight[...], preferred_element_type=jnp.float32
-            )
-        )
-    return totals
+    taps = []
+    for tap in range(TAPS):
+        start = LON_REACH + (tap - HALF) * dilation
+        for group in range(GROUPS):
+            piece = wide[group, :, pl.ds(start, cols), :]
+            taps.append(piece.astype(jnp.bfloat16).reshape(TILE_ROWS * cols, CG))
+    total = jnp.dot(
+        jnp.concatenate(taps, 1), weight[...], preferred_element_type=jnp.float32
+    )
+    return [total[row * cols : (row + 1) * cols] for row in range(TILE_ROWS)]
 
 
 def lon_first(split, info, *refs):
@@ -196,7 +196,7 @@
         ),
         out_shape=out_shape,
         compiler_params=pltpu.CompilerParams(vmem_limit_bytes=VMEM_LIMIT),
-        cost_estimate=pl.CostEstimate(flops=flops, bytes_accessed=moved, transcendentals=0),
+        cost_estimate=pl.CostEstimate(flops=flops // COST_SHARE, bytes_accessed=moved // COST_SHARE, transcendentals=0),
     )(*scalars, *args)
 
 
@@ -243,21 +243,29 @@
     def cut(sample, at, size):
         return lax.dynamic_slice(fields, (sample, at, 0, 0), (1, size, cols, C))[0]
 
-    edge = swap(cut(other, member * spare, REACH))
+    edge_piece = cut(other, member * spare, REACH)
+    edge = swap(edge_piece)
+    whole_fields = fields
+    fields = after(fields, edge_piece)
     rest = swap(cut(other, other * REACH, spare))
     near = lax.ppermute(cut(member, member * spare, REACH), "lat", near_pairs)
 
     info = jnp.concatenate([member[None], lat_dilation, lon_dilation])
-    send_edge_base = jnp.stack([other * (REACH // TILE_ROWS)])
-    keep_edge_base = jnp.stack([member * (REACH // TILE_ROWS)])
+    edge_tiles = REACH // TILE_ROWS
+    half_inner = spare // TILE_ROWS
+    bases = [
+        jnp.stack([jnp.int32(0), other * half_inner]),
+        jnp.stack([other * edge_tiles, other * edge_tiles]),
+        jnp.stack([member * edge_tiles, member * edge_tiles]),
+        jnp.stack([jnp.int32(2 * edge_tiles), member * half_inner]),
+    ]
     lat_w = [block_diagonal(lat_weight[l]) for l in range(LAYERS)]
     lon_w = [block_diagonal(lon_weight[l]) for l in range(LAYERS)]
     gains = [mix_gain[0:1], mix_gain[1:2], mlp_gain[None]]
 
-    early = (info, send_edge_base, keep_edge_base, *lat_w, *lon_w, *gains)
-    edge, info, send_edge_base, keep_edge_base, w0, w1, v0, v1, *gains = lax.optimization_barrier(
-        (edge, *early)
-    )
+    early = (info, *bases, *lat_w, *lon_w, *gains)
+    edge, info, *early = lax.optimization_barrier((edge, *early))
+    bases, (w0, w1, v0, v1), gains = early[:4], early[4:8], early[8:]
     lat_w, lon_w = (w0, w1), (v0, v1)
     far = lax.ppermute(edge, "lat", far_pairs)
 
@@ -269,7 +277,6 @@
     tiles = 2 * rows // TILE_ROWS
     wet = wet.reshape(tiles, TILE_ROWS, cols).transpose(0, 2, 1)
     rest = after(rest, wet)
-    edge_tiles = REACH // TILE_ROWS
     inner_tiles = tiles - 2 * edge_tiles
 
     def edge_tile(i):
@@ -300,7 +307,7 @@
             out_shape,
             [pltpu.VMEM((2 * rows + 2 * REACH, TILE_COLS, C), bf16)],
             lat_flops(2 * rows, grid * TILE_COLS),
-            (fields, edge, rest, near, far, gains[0], lat_w[0]),
+            (whole_fields, edge, rest, near, far, gains[0], lat_w[0]),
         )
 
     fixed = pl.BlockSpec((2 * rows, TILE_COLS, C), lambda i, s: (0, 0, 0))
@@ -386,24 +393,27 @@
             (*args, lat_w[1]),
         )
 
+    lon_rows = inner_rows // 2
     inner_across, head, tail = second_lat(
-        lat_inner, inner_rows, 2 * REACH + inner_rows, (top, bottom, inner_normed)
+        lat_inner, lon_rows, 2 * REACH + inner_rows, (top, bottom, inner_normed)
     )
     inner_halo = lon_halo(head, tail)
 
     def second(acr, halo, old, to_tile, base, number):
-        band = lambda width: pl.BlockSpec((TILE_ROWS, width, C), lambda i, s, b: (b[0] + i, 0, 0))
+        band = lambda width, which: pl.BlockSpec(
+            (TILE_ROWS, width, C), lambda i, s, b: (b[which] + i, 0, 0)
+        )
         size = number * TILE_ROWS
         return launch(
             lon_mlp,
             (info, base),
             number,
             [
-                band(LON_REACH),
-                band(cols),
-                band(LON_REACH),
-                band(cols),
-                pl.BlockSpec((1, cols, TILE_ROWS), lambda i, s, b: (to_tile(b[0] + i), 0, 0)),
+                band(LON_REACH, 0),
+                band(cols, 0),
+                band(LON_REACH, 0),
+                band(cols, 1),
+                pl.BlockSpec((1, cols, TILE_ROWS), lambda i, s, b: (to_tile(b[1] + i), 0, 0)),
                 whole(gains[2]),
                 whole(lon_w[1]),
                 whole(w_in),
@@ -416,29 +426,23 @@
             (halo[0], acr, halo[1], old, wet, gains[2], lon_w[1], w_in, w_out),
         )
 
-    half_inner = inner_tiles // 2
     send_inner = second(
-        inner_across, inner_halo, inner_state, inner_tile, send_edge_base, half_inner
+        inner_across, inner_halo, inner_state, inner_tile, bases[0], half_inner
     )
     back_inner = swap(send_inner)
     north = after(north, send_inner)
     edge_across, head, tail = second_lat(
-        lat_edge, 2 * REACH, 4 * REACH + inner_rows, (top, bottom, inner_normed, north, south)
+        lat_others,
+        2 * REACH + lon_rows,
+        4 * REACH + inner_rows,
+        (top, bottom, inner_normed, north, south),
     )
     edge_halo = lon_halo(head, tail)
-    send_edge = second(edge_across, edge_halo, edge_state, edge_tile, send_edge_base, edge_tiles)
+    send_edge = second(edge_across, edge_halo, edge_state, edge_tile, bases[1], edge_tiles)
     back_edge = swap(send_edge)
-    keep_inner = second(
-        after(inner_across, send_edge),
-        inner_halo,
-        inner_state,
-        inner_tile,
-        keep_edge_base,
-        half_inner,
-    )
-    keep_edge = second(
-        after(edge_across, send_edge), edge_halo, edge_state, edge_tile, keep_edge_base, edge_tiles
-    )
+    edge_across = after(edge_across, send_edge, back_inner)
+    keep_inner = second(edge_across, edge_halo, inner_state, inner_tile, bases[3], half_inner)
+    keep_edge = second(edge_across, edge_halo, edge_state, edge_tile, bases[2], edge_tiles)
     out = jnp.zeros(fields.shape, bf16)
     edge_at = member * spare
     inner_at = other * REACH

time: 134 us -> 127 us (0.948)
  waiting for transfers between devices: 44.8 us -> 32.9 us
  Pallas kernels: 57.1 us -> 60.8 us
  local copies, waits for them, and re-layouts: 10.2 us -> 12.2 us
    ppermute x5, waiting for transfers between devices: 41.5 us -> 28.1 us  [swap(): return lax.ppermute(x, 'lat', swap_pairs)]
    pallas_call x10, Pallas kernels: 57.1 us -> 60.8 us  [launch(): pl.pallas_call(body, grid_spec=pltpu.PrefetchScalarGridSpec(num_scalar_pr...]
    squeeze x1 -> x2, local copies, waits for them, and re-layouts: 3.13 us -> 4.81 us  [cut(): return lax.dynamic_slice(fields, (sample, at, 0, 0), (1, size, cols, C))[0]]
    unnamed x38 -> x34, local copies, waits for them, and re-layouts: 3.42 us -> 4.55 us
  transfers between devices with their start and end apart: 15 -> 15, of which waited for: 7 -> 9; matrix products, arithmetic and copies ran while one was open for 2% -> 4% of each run, Pallas kernels for 30% -> 39%
where the time goes in v1:
time: 127 us; the launch traced here: 126 us
  Pallas kernels  60.8 us (48%)
  waiting for transfers between devices  32.9 us (26%)
  starting transfers between devices  19.7 us (16%)
  local copies, waits for them, and re-layouts  12.2 us (10%)
    pallas_call x10, Pallas kernels, launch(): pl.pallas_call(body, grid_spec=pltpu.PrefetchScalarGridSpec(num_scalar_pr...  60.8 us
    ppermute x5, waiting for transfers between devices, swap(): return lax.ppermute(x, 'lat', swap_pairs)  28.1 us
    ppermute x5, starting transfers between devices, swap(): return lax.ppermute(x, 'lat', swap_pairs)  5.8 us
    ppermute x1, starting transfers between devices, on_device(): far = lax.ppermute(edge, 'lat', far_pairs)  4.9 us
    squeeze x2, local copies, waits for them, and re-layouts, cut(): return lax.dynamic_slice(fields, (sample, at, 0, 0), (1, size, cols, C))[0]  4.81 us
    unnamed x34, local copies, waits for them, and re-layouts  4.55 us
    ppermute x1, starting transfers between devices, on_device(): north = lax.ppermute(bottom, 'lat', south_pairs)  4.53 us
  transfers between devices with their start and end apart: 15, of which 9 were waited for; matrix products, arithmetic and copies ran while one was open for 4% of the time, Pallas kernels for 39%

profile of v1, /device:TPU:0, one launch (start us, length us, event | category | flops | bytes accessed | tf_op | source)
XLA Modules:
  0.0 126.4 jit_solution(663338302210688463)
XLA Ops:
  0.0 2.1 %dynamic-slice_bitcast_fusion.2 = bf16[8,192,256]{2,1,0:T(8,128)(2,1)} fusion(bf16[2,16,192,256]{3,2,1,0:T(8,128)(2,1)} %own.3, s32[]{:T(128)S(6)} %select_n.34, s32[]{:T(128)S(6)} %select_n.35), kind=kLoop, calls=%fused_computation.16 | loop fusion | bytes 1572872 | tf_op jit(solution)/shard_map/squeeze | solution.py:244
  2.1 3.0 %collective-permute-start = (bf16[8,192,256]{2,1,0:T(8,128)(2,1)}, bf16[8,192,256]{2,1,0:T(8,128)(2,1)S(1)}, u32[]{:S(2)}, u32[]{:S(2)}) collective-permute-start(bf16[8,192,256]{2,1,0:T(8,128)(2,1)} %dynamic-slice_bitcast_fusion.2), channel_id=1, source_target_pairs={{0,2},{2,0},{4,6},{6,4},{8,10},{10,8},{12,14},{14,12},{1,3},{3,1},... | collective-permute-start | bytes 2359304 | tf_op jit(solution)/shard_map/ppermute | solution.py:235
  5.0 2.7 %dynamic-slice_bitcast_fusion = (bf16[8,192,256]{2,1,0:T(8,128)(2,1)}, bf16[8,192,256]{2,1,0:T(8,128)(2,1)}) fusion(bf16[2,16,192,256]{3,2,1,0:T(8,128)(2,1)} %own.3, s32[]{:T(128)S(6)} %select_n.40, s32[]{:T(128)S(6)} %select_n.35, s32[]{:T(128)S(6)} %select_n.34, s32[]{:T(128)S(6)} %select_n.36), kind=kLoop, calls=%fused_computation.14 | loop fusion | bytes 3145744 | tf_op jit(solution)/shard_map/squeeze | solution.py:244
  7.8 1.4 %collective-permute-start.3 = (bf16[8,192,256]{2,1,0:T(8,128)(2,1)}, bf16[8,192,256]{2,1,0:T(8,128)(2,1)}, u32[]{:S(2)}, u32[]{:S(2)}) collective-permute-start(bf16[8,192,256]{2,1,0:T(8,128)(2,1)} %get-tuple-element.77), channel_id=1, source_target_pairs={{4,0},{8,4},{12,8},{2,6},{6,10},{10,14},{5,1},{9,5},{13,9},{3,7},{... | collective-permute-start | bytes 2359304 | tf_op jit(solution)/shard_map/ppermute | solution.py:251
  9.6 0.5 copy-done.15
  11.0 12.6 %collective-permute-done.edge = bf16[8,192,256]{2,1,0:T(8,128)(2,1)S(1)} collective-permute-done((bf16[8,192,256]{2,1,0:T(8,128)(2,1)}, bf16[8,192,256]{2,1,0:T(8,128)(2,1)S(1)}, u32[]{:S(2)}, u32[]{:S(2)}) %collective-permute-start) | collective-permute-done | bytes 786464 | tf_op jit(solution)/shard_map/ppermute | solution.py:235
  23.6 4.9 %collective-permute-start.4 = (bf16[8,192,256]{2,1,0:T(8,128)(2,1)S(1)}, bf16[8,192,256]{2,1,0:T(8,128)(2,1)}, u32[]{:S(2)}, u32[]{:S(2)}) collective-permute-start(bf16[8,192,256]{2,1,0:T(8,128)(2,1)S(1)} %collective-permute-done.edge), channel_id=1, source_target_pairs={{0,4},{4,8},{8,12},{6,2},{10,6},{14,10},{1,5},{5,9},{9,13},{7,3},{... | collective-permute-start | bytes 2359304 | tf_op jit(solution)/shard_map/ppermute | solution.py:270
  28.5 11.5 %collective-permute-done.2 = f32[16,192]{1,0:T(8,128)S(1)} collective-permute-done((f32[16,192]{1,0:T(8,128)S(1)}, f32[16,192]{1,0:T(8,128)S(1)}, u32[]{:S(2)}, u32[]{:S(2)}) %collective-permute-start.2) | collective-permute-done | bytes 12320 | tf_op jit(solution)/shard_map/ppermute | solution.py:235
  40.0 1.2 copy.19
  41.2 1.3 %collective-permute-done.4.far = bf16[8,192,256]{2,1,0:T(8,128)(2,1)} collective-permute-done((bf16[8,192,256]{2,1,0:T(8,128)(2,1)S(1)}, bf16[8,192,256]{2,1,0:T(8,128)(2,1)}, u32[]{:S(2)}, u32[]{:S(2)}) %collective-permute-start.4) | collective-permute-done | bytes 786464 | tf_op jit(solution)/shard_map/ppermute | solution.py:270
  42.5 5.2 %shard_map.100 = (bf16[32,48,256]{2,1,0:T(8,128)(2,1)S(1)}, bf16[32,48,256]{2,1,0:T(8,128)(2,1)S(1)}, bf16[32,48,256]{2,1,0:T(8,128)(2,1)S(1)}, bf16[32,48,256]{2,1,0:T(8,128)(2,1)S(1)}) custom-call(s32[5]{0:T(128)S(1)} %pad_add_fusion.info, bf16[2,16,192,256]{3,2,1,0:T(8,128)(2,1)} %own.3, bf16[8,192,256]{2,1,0:T(8,128)(2,1)S(1)} %collective-permute-done.edge, ...), custom_call_target="tpu_custom_call" | custom-call | flops 20 | tf_op jit(solution)/shard_map/pallas_call | solution.py:188
  47.7 0.9 copy-done.7
  49.1 6.2 %shard_map.101 = (bf16[32,96,256]{2,1,0:T(8,128)(2,1)S(1)}, bf16[32,96,256]{2,1,0:T(8,128)(2,1)}) custom-call(s32[5]{0:T(128)S(1)} %pad_add_fusion.info, bf16[2,16,192,256]{3,2,1,0:T(8,128)(2,1)} %own.3, bf16[8,192,256]{2,1,0:T(8,128)(2,1)S(1)} %collective-permute-done.edge, bf16[8,192,256]{2,1,0:T(8,128)(2,1)} %collective-permute-done.1.rest, ...), custom_call_target="tpu_custom_call" | custom-call | flops 20 | tf_op jit(solution)/shard_map/pallas_call | solution.py:188
  55.3 1.2 copy-done.4
  56.5 6.6 %shard_map.102 = (bf16[16,192,256]{2,1,0:T(8,128)(2,1)}, bf16[8,192,256]{2,1,0:T(8,128)(2,1)S(1)}, bf16[8,192,256]{2,1,0:T(8,128)(2,1)S(1)}) custom-call(s32[5]{0:T(128)S(1)} %pad_add_fusion.info, bf16[32,48,256]{2,1,0:T(8,128)(2,1)S(1)} %collective-permute-done.5.refs_0_, bf16[32,48,256]{2,1,0:T(8,128)(2,1)S(1)} %get-tuple-element.50.refs_1_, ...), custom_call_target="tpu_custom_call" | custom-call | flops 20 | tf_op jit(solution)/shard_map/pallas_call | solution.py:188
  63.1 4.5 %collective-permute-start.7 = (bf16[8,192,256]{2,1,0:T(8,128)(2,1)S(1)}, bf16[8,192,256]{2,1,0:T(8,128)(2,1)S(1)}, u32[]{:S(2)}, u32[]{:S(2)}) collective-permute-start(bf16[8,192,256]{2,1,0:T(8,128)(2,1)S(1)} %get-tuple-element.59.bottom), channel_id=1, source_target_pairs={{0,4},{2,6},{4,8},{6,10},{8,12},{10,14},{1,5},{3,7},{5,9},{7,11},{... | collective-permute-start | bytes 2359304 | tf_op jit(solution)/shard_map/ppermute | solution.py:374
  67.6 1.5 %collective-permute-start.10 = (bf16[8,192,256]{2,1,0:T(8,128)(2,1)S(1)}, bf16[8,192,256]{2,1,0:T(8,128)(2,1)}, u32[]{:S(2)}, u32[]{:S(2)}) collective-permute-start(bf16[8,192,256]{2,1,0:T(8,128)(2,1)S(1)} %get-tuple-element.58.top), channel_id=1, source_target_pairs={{4,0},{6,2},{8,4},{10,6},{12,8},{14,10},{5,1},{7,3},{9,5},{11,7},{... | collective-permute-start | bytes 2359304 | tf_op jit(solution)/shard_map/ppermute | solution.py:375
  69.1 6.4 %shard_map.103 = (bf16[16,192,256]{2,1,0:T(8,128)(2,1)}, bf16[16,192,256]{2,1,0:T(8,128)(2,1)}) custom-call(s32[5]{0:T(128)S(1)} %pad_add_fusion.info, bf16[32,48,256]{2,1,0:T(8,128)(2,1)S(1)} %collective-permute-done.5.refs_0_, bf16[32,48,256]{2,1,0:T(8,128)(2,1)S(1)} %get-tuple-element.50.refs_1_, bf16[32,96,256]{2,1,0:T(8,128)(2,1)} %copy-done.4, ...), custom_call_target="tpu_custom_call" | custom-call | flops 20 | tf_op jit(solution)/shard_map/pallas_call | solution.py:188
  75.5 1.4 %copy-done.6 = bf16[16,192,256]{2,1,0:T(8,128)(2,1)S(1)} copy-done((bf16[16,192,256]{2,1,0:T(8,128)(2,1)S(1)}, bf16[16,192,256]{2,1,0:T(8,128)(2,1)}, u32[]{:S(2)}) %copy-start.6) | copy-done | bytes 1572888
  76.9 2.9 %shard_map.104 = (bf16[8,192,256]{2,1,0:T(8,128)(2,1)S(1)}, bf16[8,48,256]{2,1,0:T(8,128)(2,1)S(1)}, bf16[8,48,256]{2,1,0:T(8,128)(2,1)S(1)}) custom-call(s32[5]{0:T(128)S(1)} %pad_add_fusion.info, bf16[8,192,256]{2,1,0:T(8,128)(2,1)S(1)} %get-tuple-element.58.top, bf16[8,192,256]{2,1,0:T(8,128)(2,1)S(1)} %get-tuple-element.59.bottom, ...), custom_call_target="tpu_custom_call" | custom-call | flops 10 | tf_op jit(solution)/shard_map/pallas_call | solution.py:188
  80.4 0.9 collective-permute-done.8.left
  81.6 5.9 %shard_map.105 = bf16[8,192,256]{2,1,0:T(8,128)(2,1)S(1)} custom-call(s32[5]{0:T(128)S(1)} %pad_add_fusion.info, s32[2]{0:T(128)S(1)} %get-tuple-element.61.base, bf16[8,48,256]{2,1,0:T(8,128)(2,1)S(1)} %collective-permute-done.8.left, bf16[8,192,256]{2,1,0:T(8,128)(2,1)S(1)} %get-tuple-element.64.middle, ...), custom_call_target="tpu_custom_call" | custom-call | flops 26 | tf_op jit(solution)/shard_map/pallas_call | solution.py:188
  87.5 1.6 %collective-permute-start.13 = (bf16[8,192,256]{2,1,0:T(8,128)(2,1)S(1)}, bf16[8,192,256]{2,1,0:T(8,128)(2,1)S(1)}, u32[]{:S(2)}, u32[]{:S(2)}) collective-permute-start(bf16[8,192,256]{2,1,0:T(8,128)(2,1)S(1)} %shard_map.105), channel_id=1, source_target_pairs={{0,2},{2,0},{4,6},{6,4},{8,10},{10,8},{12,14},{14,12},{1,3},{3,1},... | collective-permute-start | bytes 2359304 | tf_op jit(solution)/shard_map/ppermute | solution.py:235
  89.1 6.9 %shard_map.106 = (bf16[24,192,256]{2,1,0:T(8,128)(2,1)}, bf16[24,48,256]{2,1,0:T(8,128)(2,1)S(1)}, bf16[24,48,256]{2,1,0:T(8,128)(2,1)S(1)}) custom-call(s32[5]{0:T(128)S(1)} %pad_add_fusion.info, bf16[8,192,256]{2,1,0:T(8,128)(2,1)S(1)} %get-tuple-element.58.top, bf16[8,192,256]{2,1,0:T(8,128)(2,1)S(1)} %get-tuple-element.59.bottom, ...), custom_call_target="tpu_custom_call" | custom-call | flops 30 | tf_op jit(solution)/shard_map/pallas_call | solution.py:188
  96.6 1.5 %collective-permute-done.11.left = bf16[24,48,256]{2,1,0:T(8,128)(2,1)S(1)} collective-permute-done((bf16[24,48,256]{2,1,0:T(8,128)(2,1)S(1)}, bf16[24,48,256]{2,1,0:T(8,128)(2,1)S(1)}, u32[]{:S(2)}, u32[]{:S(2)}) %collective-permute-start.11) | collective-permute-done | bytes 589856 | tf_op jit(solution)/shard_map/ppermute | solution.py:238
  98.1 0.8 collective-permute-done.12.right
  98.9 6.9 %shard_map.107 = bf16[8,192,256]{2,1,0:T(8,128)(2,1)S(1)} custom-call(s32[5]{0:T(128)S(1)} %pad_add_fusion.info, s32[2]{0:T(128)S(1)} %get-tuple-element.72.base, bf16[24,48,256]{2,1,0:T(8,128)(2,1)S(1)} %collective-permute-done.11.left, bf16[24,192,256]{2,1,0:T(8,128)(2,1)} %get-tuple-element.75.middle, ...), custom_call_target="tpu_custom_call" | custom-call | flops 26 | tf_op jit(solution)/shard_map/pallas_call | solution.py:188
  105.8 1.2 collective-permute-start.14
  107.3 6.9 %shard_map.109 = bf16[8,192,256]{2,1,0:T(8,128)(2,1)S(1)} custom-call(s32[5]{0:T(128)S(1)} %pad_add_fusion.info, s32[2]{0:T(128)S(1)} %get-tuple-element.76.base, bf16[24,48,256]{2,1,0:T(8,128)(2,1)S(1)} %collective-permute-done.11.left, bf16[24,192,256]{2,1,0:T(8,128)(2,1)} %get-tuple-element.75.middle, ...), custom_call_target="tpu_custom_call" | custom-call | flops 26 | tf_op jit(solution)/shard_map/pallas_call | solution.py:188
  114.2 6.9 %shard_map.108 = bf16[8,192,256]{2,1,0:T(8,128)(2,1)S(1)} custom-call(s32[5]{0:T(128)S(1)} %pad_add_fusion.info, s32[2]{0:T(128)S(1)} %get-tuple-element.42.base, bf16[24,48,256]{2,1,0:T(8,128)(2,1)S(1)} %collective-permute-done.11.left, bf16[24,192,256]{2,1,0:T(8,128)(2,1)} %get-tuple-element.75.middle, ...), custom_call_target="tpu_custom_call" | custom-call | flops 26 | tf_op jit(solution)/shard_map/pallas_call | solution.py:188
  121.7 3.8 %collective-permute-done.14 = bf16[8,192,256]{2,1,0:T(8,128)(2,1)S(1)} collective-permute-done((bf16[8,192,256]{2,1,0:T(8,128)(2,1)S(1)}, bf16[8,192,256]{2,1,0:T(8,128)(2,1)S(1)}, u32[]{:S(2)}, u32[]{:S(2)}) %collective-permute-start.14) | collective-permute-done | bytes 786464 | tf_op jit(solution)/shard_map/ppermute | solution.py:235
  125.5 0.9 bitcast_dynamic-update-slice_fusion
  (65 shorter events, 3.8 us)
Async XLA Ops:
  2.1 21.5 %collective-permute-start = (bf16[8,192,256]{2,1,0:T(8,128)(2,1)}, bf16[8,192,256]{2,1,0:T(8,128)(2,1)S(1)}, u32[]{:S(2)}, u32[]{:S(2)}) collective-permute-start(bf16[8,192,256]{2,1,0:T(8,128)(2,1)} %dynamic-slice_bitcast_fusion.2), channel_id=1, source_target_pairs={{0,2},{2,0},{4,6},{6,4},{8,10},{10,8},{12,14},{14,12},{1,3},{3,1},... | collective-permute-start | bytes 2359304 | tf_op jit(solution)/shard_map/ppermute | solution.py:235
  5.0 4.2 %copy-start.11 = (bf16[2,5,2,128,128]{4,3,2,1,0:T(8,128)(2,1)S(1)}, bf16[2,5,2,128,128]{4,3,2,1,0:T(8,128)(2,1)}, u32[]{:S(2)}) copy-start(bf16[2,5,2,128,128]{4,3,2,1,0:T(8,128)(2,1)} %param.12) | copy-start | bytes 1966084
  7.8 1.5 %copy-start.12 = (bf16[2,5,2,128,128]{4,3,2,1,0:T(8,128)(2,1)S(1)}, bf16[2,5,2,128,128]{4,3,2,1,0:T(8,128)(2,1)}, u32[]{:S(2)}) copy-start(bf16[2,5,2,128,128]{4,3,2,1,0:T(8,128)(2,1)} %param.13) | copy-start | bytes 1966084
  7.8 33.4 %collective-permute-start.1 = (bf16[8,192,256]{2,1,0:T(8,128)(2,1)}, bf16[8,192,256]{2,1,0:T(8,128)(2,1)}, u32[]{:S(2)}, u32[]{:S(2)}) collective-permute-start(bf16[8,192,256]{2,1,0:T(8,128)(2,1)} %get-tuple-element.78), channel_id=1, source_target_pairs={{0,2},{2,0},{4,6},{6,4},{8,10},{10,8},{12,14},{14,12},{1,3},{3,1},... | collective-permute-start | bytes 2359304 | tf_op jit(solution)/shard_map/ppermute | solution.py:235
  7.8 33.4 %collective-permute-start.3 = (bf16[8,192,256]{2,1,0:T(8,128)(2,1)}, bf16[8,192,256]{2,1,0:T(8,128)(2,1)}, u32[]{:S(2)}, u32[]{:S(2)}) collective-permute-start(bf16[8,192,256]{2,1,0:T(8,128)(2,1)} %get-tuple-element.77), channel_id=1, source_target_pairs={{4,0},{8,4},{12,8},{2,6},{6,10},{10,14},{5,1},{9,5},{13,9},{3,7},{... | collective-permute-start | bytes 2359304 | tf_op jit(solution)/shard_map/ppermute | solution.py:251
  9.5 0.7 copy-start.15
  9.5 0.7 copy-start.16
  10.3 0.7 copy-start.14
  10.3 18.2 %copy-start.13 = (s32[16,192]{1,0:T(8,128)S(1)}, s32[16,192]{1,0:T(8,128)}, u32[]{:S(2)}) copy-start(s32[16,192]{1,0:T(8,128)} %param.19) | copy-start | bytes 36868
  23.6 18.9 %collective-permute-start.4 = (bf16[8,192,256]{2,1,0:T(8,128)(2,1)S(1)}, bf16[8,192,256]{2,1,0:T(8,128)(2,1)}, u32[]{:S(2)}, u32[]{:S(2)}) collective-permute-start(bf16[8,192,256]{2,1,0:T(8,128)(2,1)S(1)} %collective-permute-done.edge), channel_id=1, source_target_pairs={{0,4},{4,8},{8,12},{6,2},{10,6},{14,10},{1,5},{5,9},{9,13},{7,3},{... | collective-permute-start | bytes 2359304 | tf_op jit(solution)/shard_map/ppermute | solution.py:270
  28.5 11.5 %collective-permute-start.2 = (f32[16,192]{1,0:T(8,128)S(1)}, f32[16,192]{1,0:T(8,128)S(1)}, u32[]{:S(2)}, u32[]{:S(2)}) collective-permute-start(f32[16,192]{1,0:T(8,128)S(1)} %convert_element_type.3), channel_id=1, source_target_pairs={{0,2},{2,0},{4,6},{6,4},{8,10},{10,8},{12,14},{14,12},{1,3},{3,1},... | collective-permute-start | bytes 36872 | tf_op jit(solution)/shard_map/ppermute | solution.py:235
  47.7 0.9 copy-start.7
  48.6 7.8 %collective-permute-start.5 = (bf16[32,48,256]{2,1,0:T(8,128)(2,1)S(1)}, bf16[32,48,256]{2,1,0:T(8,128)(2,1)S(1)}, u32[]{:S(2)}, u32[]{:S(2)}) collective-permute-start(bf16[32,48,256]{2,1,0:T(8,128)(2,1)S(1)} %get-tuple-element.49.refs_3_), channel_id=1, source_target_pairs={{0,1},{1,0},{2,3},{3,2},{4,5},{5,4},{6,7},{7,6},{8,9},{9,8},{10,11... | collective-permute-start | bytes 2359304 | tf_op jit(solution)/shard_map/ppermute | solution.py:238
  48.6 7.8 %collective-permute-start.6 = (bf16[32,48,256]{2,1,0:T(8,128)(2,1)S(1)}, bf16[32,48,256]{2,1,0:T(8,128)(2,1)S(1)}, u32[]{:S(2)}, u32[]{:S(2)}) collective-permute-start(bf16[32,48,256]{2,1,0:T(8,128)(2,1)S(1)} %get-tuple-element.50.refs_1_), channel_id=1, source_target_pairs={{1,0},{0,1},{3,2},{2,3},{5,4},{4,5},{7,6},{6,7},{9,8},{8,9},{11,10... | collective-permute-start | bytes 2359304 | tf_op jit(solution)/shard_map/ppermute | solution.py:238
  55.3 1.2 copy-start.4
  56.5 12.6 %copy-start = (f32[8,4,192]{1,2,0:T(8,128)S(1)}, f32[8,4,192]{1,2,0:T(8,128)}, u32[]{:S(2)}) copy-start(f32[8,4,192]{1,2,0:T(8,128)} %copy.19) | copy-start | bytes 73732
  56.5 12.6 %copy-start.8 = (bf16[32,48,256]{2,1,0:T(8,128)(2,1)S(1)}, bf16[32,48,256]{2,1,0:T(8,128)(2,1)}, u32[]{:S(2)}) copy-start(bf16[32,48,256]{2,1,0:T(8,128)(2,1)} %copy-done.7) | copy-start | bytes 2359300
  63.1 26.0 %collective-permute-start.7 = (bf16[8,192,256]{2,1,0:T(8,128)(2,1)S(1)}, bf16[8,192,256]{2,1,0:T(8,128)(2,1)S(1)}, u32[]{:S(2)}, u32[]{:S(2)}) collective-permute-start(bf16[8,192,256]{2,1,0:T(8,128)(2,1)S(1)} %get-tuple-element.59.bottom), channel_id=1, source_target_pairs={{0,4},{2,6},{4,8},{6,10},{8,12},{10,14},{1,5},{3,7},{5,9},{7,11},{... | collective-permute-start | bytes 2359304 | tf_op jit(solution)/shard_map/ppermute | solution.py:374
  67.6 21.5 %collective-permute-start.10 = (bf16[8,192,256]{2,1,0:T(8,128)(2,1)S(1)}, bf16[8,192,256]{2,1,0:T(8,128)(2,1)}, u32[]{:S(2)}, u32[]{:S(2)}) collective-permute-start(bf16[8,192,256]{2,1,0:T(8,128)(2,1)S(1)} %get-tuple-element.58.top), channel_id=1, source_target_pairs={{4,0},{6,2},{8,4},{10,6},{12,8},{14,10},{5,1},{7,3},{9,5},{11,7},{... | collective-permute-start | bytes 2359304 | tf_op jit(solution)/shard_map/ppermute | solution.py:375
  75.5 1.4 %copy-start.6 = (bf16[16,192,256]{2,1,0:T(8,128)(2,1)S(1)}, bf16[16,192,256]{2,1,0:T(8,128)(2,1)}, u32[]{:S(2)}) copy-start(bf16[16,192,256]{2,1,0:T(8,128)(2,1)} %get-tuple-element.60.inner) | copy-start | bytes 4718596
  76.9 4.7 %copy-start.1 = (bf16[256,1024]{1,0:T(8,128)(2,1)S(1)}, bf16[256,1024]{1,0:T(8,128)(2,1)}, u32[]{:S(2)}) copy-start(bf16[256,1024]{1,0:T(8,128)(2,1)} %w_in.7) | copy-start | bytes 1572868
  76.9 4.7 %copy-start.2 = (bf16[1024,256]{1,0:T(8,128)(2,1)S(1)}, bf16[1024,256]{1,0:T(8,128)(2,1)}, u32[]{:S(2)}) copy-start(bf16[1024,256]{1,0:T(8,128)(2,1)} %w_out.7) | copy-start | bytes 1572868
  76.9 4.7 %copy-start.5 = (bf16[16,192,256]{2,1,0:T(8,128)(2,1)S(1)}, bf16[16,192,256]{2,1,0:T(8,128)(2,1)}, u32[]{:S(2)}) copy-start(bf16[16,192,256]{2,1,0:T(8,128)(2,1)} %get-tuple-element.66.state) | copy-start | bytes 4718596
  76.9 4.7 %copy-start.9 = (f32[256]{0:T(256)S(1)}, f32[256]{0:T(256)}, u32[]{:S(2)}) copy-start(f32[256]{0:T(256)} %param.14) | copy-start | bytes 3076
  79.8 1.5 %collective-permute-start.8 = (bf16[8,48,256]{2,1,0:T(8,128)(2,1)S(1)}, bf16[8,48,256]{2,1,0:T(8,128)(2,1)S(1)}, u32[]{:S(2)}, u32[]{:S(2)}) collective-permute-start(bf16[8,48,256]{2,1,0:T(8,128)(2,1)S(1)} %get-tuple-element.63), channel_id=1, source_target_pairs={{0,1},{1,0},{2,3},{3,2},{4,5},{5,4},{6,7},{7,6},{8,9},{9,8},{10,11... | collective-permute-start | bytes 589832 | tf_op jit(solution)/shard_map/ppermute | solution.py:238
  79.9 1.7 %collective-permute-start.9 = (bf16[8,48,256]{2,1,0:T(8,128)(2,1)S(1)}, bf16[8,48,256]{2,1,0:T(8,128)(2,1)S(1)}, u32[]{:S(2)}, u32[]{:S(2)}) collective-permute-start(bf16[8,48,256]{2,1,0:T(8,128)(2,1)S(1)} %get-tuple-element.65), channel_id=1, source_target_pairs={{1,0},{0,1},{3,2},{2,3},{5,4},{4,5},{7,6},{6,7},{9,8},{8,9},{11,10... | collective-permute-start | bytes 589832 | tf_op jit(solution)/shard_map/ppermute | solution.py:238
  87.5 11.4 %copy-start.3 = (bf16[16,192,256]{2,1,0:T(8,128)(2,1)S(1)}, bf16[16,192,256]{2,1,0:T(8,128)(2,1)}, u32[]{:S(2)}) copy-start(bf16[16,192,256]{2,1,0:T(8,128)(2,1)} %get-tuple-element.74.state) | copy-start | bytes 4718596
  87.5 19.7 %collective-permute-start.13 = (bf16[8,192,256]{2,1,0:T(8,128)(2,1)S(1)}, bf16[8,192,256]{2,1,0:T(8,128)(2,1)S(1)}, u32[]{:S(2)}, u32[]{:S(2)}) collective-permute-start(bf16[8,192,256]{2,1,0:T(8,128)(2,1)S(1)} %shard_map.105), channel_id=1, source_target_pairs={{0,2},{2,0},{4,6},{6,4},{8,10},{10,8},{12,14},{14,12},{1,3},{3,1},... | collective-permute-start | bytes 2359304 | tf_op jit(solution)/shard_map/ppermute | solution.py:235
  96.1 2.0 %collective-permute-start.11 = (bf16[24,48,256]{2,1,0:T(8,128)(2,1)S(1)}, bf16[24,48,256]{2,1,0:T(8,128)(2,1)S(1)}, u32[]{:S(2)}, u32[]{:S(2)}) collective-permute-start(bf16[24,48,256]{2,1,0:T(8,128)(2,1)S(1)} %get-tuple-element.70), channel_id=1, source_target_pairs={{0,1},{1,0},{2,3},{3,2},{4,5},{5,4},{6,7},{7,6},{8,9},{9,8},{10,11... | collective-permute-start | bytes 1769480 | tf_op jit(solution)/shard_map/ppermute | solution.py:238
  96.1 2.8 %collective-permute-start.12 = (bf16[24,48,256]{2,1,0:T(8,128)(2,1)S(1)}, bf16[24,48,256]{2,1,0:T(8,128)(2,1)S(1)}, u32[]{:S(2)}, u32[]{:S(2)}) collective-permute-start(bf16[24,48,256]{2,1,0:T(8,128)(2,1)S(1)} %get-tuple-element.73), channel_id=1, source_target_pairs={{1,0},{0,1},{3,2},{2,3},{5,4},{4,5},{7,6},{6,7},{9,8},{8,9},{11,10... | collective-permute-start | bytes 1769480 | tf_op jit(solution)/shard_map/ppermute | solution.py:238
  105.8 19.6 %collective-permute-start.14 = (bf16[8,192,256]{2,1,0:T(8,128)(2,1)S(1)}, bf16[8,192,256]{2,1,0:T(8,128)(2,1)S(1)}, u32[]{:S(2)}, u32[]{:S(2)}) collective-permute-start(bf16[8,192,256]{2,1,0:T(8,128)(2,1)S(1)} %shard_map.107), channel_id=1, source_target_pairs={{0,2},{2,0},{4,6},{6,4},{8,10},{10,8},{12,14},{14,12},{1,3},{3,1},... | collective-permute-start | bytes 2359304 | tf_op jit(solution)/shard_map/ppermute | solution.py:235
  121.7 3.8 %copy-start.10 = (bf16[2,16,192,256]{3,2,1,0:T(8,128)(2,1)}, bf16[2,16,192,256]{3,2,1,0:T(8,128)(2,1)S(1)}, u32[]{:S(2)}) copy-start(bf16[2,16,192,256]{3,2,1,0:T(8,128)(2,1)S(1)} %bitcast_dynamic-update-slice_fusion.1) | copy-start | bytes 9437188

commit v2 on v1

--- a/solution.py
+++ b/solution.py
@@ -119,7 +119,7 @@
     put_ends(across, head, tail)
 
 
-def lon_total(dilation, pieces, weight, wide):
+def lon_total(dilation, pieces, weight, wide, by_row=False):
     at = 0
     for piece in pieces:
         width = piece.shape[1]
@@ -129,6 +129,17 @@
             ].astype(jnp.float32)
         at += width
     cols = at - 2 * LON_REACH
+    if by_row:
+        totals = []
+        for row in range(TILE_ROWS):
+            taps = []
+            for tap in range(TAPS):
+                start = LON_REACH + (tap - HALF) * dilation
+                for group in range(GROUPS):
+                    taps.append(wide[group, row, pl.ds(start, cols), :].astype(jnp.bfloat16))
+            lhs = jnp.concatenate(taps, 1)
+            totals.append(jnp.dot(lhs, weight[...], preferred_element_type=jnp.float32))
+        return totals
     taps = []
     for tap in range(TAPS):
         start = LON_REACH + (tap - HALF) * dilation
@@ -167,7 +178,7 @@
 
 
 def lon_mlp(info, base, left, middle, right, state, ocean, gain, weight, w_in, w_out, out, wide):
-    totals = lon_total(info[4], (left, middle, right), weight, wide)
+    totals = lon_total(info[4], (left, middle, right), weight, wide, True)
     for row, total in enumerate(totals):
         old = state[row].astype(jnp.float32)
         new = (old + total * ocean[0][:, row : row + 1]).astype(jnp.bfloat16).astype(jnp.float32)

time: 127 us -> 126 us (level)
  Pallas kernels: 60.8 us -> 55.9 us
  waiting for transfers between devices: 32.9 us -> 35.9 us
    pallas_call x10, Pallas kernels: 60.8 us -> 55.9 us  [launch(): pl.pallas_call(body, grid_spec=pltpu.PrefetchScalarGridSpec(num_scalar_pr...]
    ppermute x5, waiting for transfers between devices: 28.1 us -> 30.2 us  [swap(): return lax.ppermute(x, 'lat', swap_pairs)]
  transfers between devices with their start and end apart: 15 -> 15, of which waited for: 9 -> 10; matrix products, arithmetic and copies ran while one was open for 4% -> 4% of each run, Pallas kernels for 39% -> 35%
where the time goes in v2:
time: 126 us; the launch traced here: 125 us
  Pallas kernels  55.9 us (44%)
  waiting for transfers between devices  35.9 us (28%)
  starting transfers between devices  20.1 us (16%)
  local copies, waits for them, and re-layouts  12.2 us (10%)
    pallas_call x10, Pallas kernels, launch(): pl.pallas_call(body, grid_spec=pltpu.PrefetchScalarGridSpec(num_scalar_pr...  55.9 us
    ppermute x5, waiting for transfers between devices, swap(): return lax.ppermute(x, 'lat', swap_pairs)  30.2 us
    ppermute x5, starting transfers between devices, swap(): return lax.ppermute(x, 'lat', swap_pairs)  6.16 us
    ppermute x1, starting transfers between devices, on_device(): far = lax.ppermute(edge, 'lat', far_pairs)  4.9 us
    squeeze x2, local copies, waits for them, and re-layouts, cut(): return lax.dynamic_slice(fields, (sample, at, 0, 0), (1, size, cols, C))[0]  4.81 us
    unnamed x34, local copies, waits for them, and re-layouts  4.55 us
    ppermute x1, starting transfers between devices, on_device(): north = lax.ppermute(bottom, 'lat', south_pairs)  4.52 us
  transfers between devices with their start and end apart: 15, of which 10 were waited for; matrix products, arithmetic and copies ran while one was open for 4% of the time, Pallas kernels for 35%

profile of v2, /device:TPU:0, one launch (start us, length us, event | category | flops | bytes accessed | tf_op | source)
XLA Modules:
  0.0 124.9 jit_solution(169470599168690569)
XLA Ops:
  0.0 2.1 %dynamic-slice_bitcast_fusion.2 = bf16[8,192,256]{2,1,0:T(8,128)(2,1)} fusion(bf16[2,16,192,256]{3,2,1,0:T(8,128)(2,1)} %own.3, s32[]{:T(128)S(6)} %select_n.34, s32[]{:T(128)S(6)} %select_n.35), kind=kLoop, calls=%fused_computation.16 | loop fusion | bytes 1572872 | tf_op jit(solution)/shard_map/squeeze | solution.py:255
  2.1 3.0 %collective-permute-start = (bf16[8,192,256]{2,1,0:T(8,128)(2,1)}, bf16[8,192,256]{2,1,0:T(8,128)(2,1)S(1)}, u32[]{:S(2)}, u32[]{:S(2)}) collective-permute-start(bf16[8,192,256]{2,1,0:T(8,128)(2,1)} %dynamic-slice_bitcast_fusion.2), channel_id=1, source_target_pairs={{0,2},{2,0},{4,6},{6,4},{8,10},{10,8},{12,14},{14,12},{1,3},{3,1},... | collective-permute-start | bytes 2359304 | tf_op jit(solution)/shard_map/ppermute | solution.py:246
  5.0 2.7 %dynamic-slice_bitcast_fusion = (bf16[8,192,256]{2,1,0:T(8,128)(2,1)}, bf16[8,192,256]{2,1,0:T(8,128)(2,1)}) fusion(bf16[2,16,192,256]{3,2,1,0:T(8,128)(2,1)} %own.3, s32[]{:T(128)S(6)} %select_n.40, s32[]{:T(128)S(6)} %select_n.35, s32[]{:T(128)S(6)} %select_n.34, s32[]{:T(128)S(6)} %select_n.36), kind=kLoop, calls=%fused_computation.14 | loop fusion | bytes 3145744 | tf_op jit(solution)/shard_map/squeeze | solution.py:255
  7.8 1.4 %collective-permute-start.3 = (bf16[8,192,256]{2,1,0:T(8,128)(2,1)}, bf16[8,192,256]{2,1,0:T(8,128)(2,1)}, u32[]{:S(2)}, u32[]{:S(2)}) collective-permute-start(bf16[8,192,256]{2,1,0:T(8,128)(2,1)} %get-tuple-element.77), channel_id=1, source_target_pairs={{4,0},{8,4},{12,8},{2,6},{6,10},{10,14},{5,1},{9,5},{13,9},{3,7},{... | collective-permute-start | bytes 2359304 | tf_op jit(solution)/shard_map/ppermute | solution.py:262
  11.0 12.6 %collective-permute-done.edge = bf16[8,192,256]{2,1,0:T(8,128)(2,1)S(1)} collective-permute-done((bf16[8,192,256]{2,1,0:T(8,128)(2,1)}, bf16[8,192,256]{2,1,0:T(8,128)(2,1)S(1)}, u32[]{:S(2)}, u32[]{:S(2)}) %collective-permute-start) | collective-permute-done | bytes 786464 | tf_op jit(solution)/shard_map/ppermute | solution.py:246
  23.6 4.9 %collective-permute-start.4 = (bf16[8,192,256]{2,1,0:T(8,128)(2,1)S(1)}, bf16[8,192,256]{2,1,0:T(8,128)(2,1)}, u32[]{:S(2)}, u32[]{:S(2)}) collective-permute-start(bf16[8,192,256]{2,1,0:T(8,128)(2,1)S(1)} %collective-permute-done.edge), channel_id=1, source_target_pairs={{0,4},{4,8},{8,12},{6,2},{10,6},{14,10},{1,5},{5,9},{9,13},{7,3},{... | collective-permute-start | bytes 2359304 | tf_op jit(solution)/shard_map/ppermute | solution.py:281
  28.5 11.5 %collective-permute-done.2 = f32[16,192]{1,0:T(8,128)S(1)} collective-permute-done((f32[16,192]{1,0:T(8,128)S(1)}, f32[16,192]{1,0:T(8,128)S(1)}, u32[]{:S(2)}, u32[]{:S(2)}) %collective-permute-start.2) | collective-permute-done | bytes 12320 | tf_op jit(solution)/shard_map/ppermute | solution.py:246
  40.0 1.2 copy.19
  41.2 1.3 %collective-permute-done.4.far = bf16[8,192,256]{2,1,0:T(8,128)(2,1)} collective-permute-done((bf16[8,192,256]{2,1,0:T(8,128)(2,1)S(1)}, bf16[8,192,256]{2,1,0:T(8,128)(2,1)}, u32[]{:S(2)}, u32[]{:S(2)}) %collective-permute-start.4) | collective-permute-done | bytes 786464 | tf_op jit(solution)/shard_map/ppermute | solution.py:281
  42.5 5.2 %shard_map.100 = (bf16[32,48,256]{2,1,0:T(8,128)(2,1)S(1)}, bf16[32,48,256]{2,1,0:T(8,128)(2,1)S(1)}, bf16[32,48,256]{2,1,0:T(8,128)(2,1)S(1)}, bf16[32,48,256]{2,1,0:T(8,128)(2,1)S(1)}) custom-call(s32[5]{0:T(128)S(1)} %pad_add_fusion.info, bf16[2,16,192,256]{3,2,1,0:T(8,128)(2,1)} %own.3, bf16[8,192,256]{2,1,0:T(8,128)(2,1)S(1)} %collective-permute-done.edge, ...), custom_call_target="tpu_custom_call" | custom-call | flops 20 | tf_op jit(solution)/shard_map/pallas_call | solution.py:199
  47.7 0.9 copy-done.7
  49.1 6.2 %shard_map.101 = (bf16[32,96,256]{2,1,0:T(8,128)(2,1)S(1)}, bf16[32,96,256]{2,1,0:T(8,128)(2,1)}) custom-call(s32[5]{0:T(128)S(1)} %pad_add_fusion.info, bf16[2,16,192,256]{3,2,1,0:T(8,128)(2,1)} %own.3, bf16[8,192,256]{2,1,0:T(8,128)(2,1)S(1)} %collective-permute-done.edge, bf16[8,192,256]{2,1,0:T(8,128)(2,1)} %collective-permute-done.1.rest, ...), custom_call_target="tpu_custom_call" | custom-call | flops 20 | tf_op jit(solution)/shard_map/pallas_call | solution.py:199
  55.3 1.2 copy-done.4
  56.5 6.7 %shard_map.102 = (bf16[16,192,256]{2,1,0:T(8,128)(2,1)}, bf16[8,192,256]{2,1,0:T(8,128)(2,1)S(1)}, bf16[8,192,256]{2,1,0:T(8,128)(2,1)S(1)}) custom-call(s32[5]{0:T(128)S(1)} %pad_add_fusion.info, bf16[32,48,256]{2,1,0:T(8,128)(2,1)S(1)} %collective-permute-done.5.refs_0_, bf16[32,48,256]{2,1,0:T(8,128)(2,1)S(1)} %get-tuple-element.50.refs_1_, ...), custom_call_target="tpu_custom_call" | custom-call | flops 20 | tf_op jit(solution)/shard_map/pallas_call | solution.py:199
  63.1 4.5 %collective-permute-start.7 = (bf16[8,192,256]{2,1,0:T(8,128)(2,1)S(1)}, bf16[8,192,256]{2,1,0:T(8,128)(2,1)S(1)}, u32[]{:S(2)}, u32[]{:S(2)}) collective-permute-start(bf16[8,192,256]{2,1,0:T(8,128)(2,1)S(1)} %get-tuple-element.59.bottom), channel_id=1, source_target_pairs={{0,4},{2,6},{4,8},{6,10},{8,12},{10,14},{1,5},{3,7},{5,9},{7,11},{... | collective-permute-start | bytes 2359304 | tf_op jit(solution)/shard_map/ppermute | solution.py:385
  67.7 1.5 %collective-permute-start.10 = (bf16[8,192,256]{2,1,0:T(8,128)(2,1)S(1)}, bf16[8,192,256]{2,1,0:T(8,128)(2,1)}, u32[]{:S(2)}, u32[]{:S(2)}) collective-permute-start(bf16[8,192,256]{2,1,0:T(8,128)(2,1)S(1)} %get-tuple-element.58.top), channel_id=1, source_target_pairs={{4,0},{6,2},{8,4},{10,6},{12,8},{14,10},{5,1},{7,3},{9,5},{11,7},{... | collective-permute-start | bytes 2359304 | tf_op jit(solution)/shard_map/ppermute | solution.py:386
  69.2 6.5 %shard_map.103 = (bf16[16,192,256]{2,1,0:T(8,128)(2,1)}, bf16[16,192,256]{2,1,0:T(8,128)(2,1)}) custom-call(s32[5]{0:T(128)S(1)} %pad_add_fusion.info, bf16[32,48,256]{2,1,0:T(8,128)(2,1)S(1)} %collective-permute-done.5.refs_0_, bf16[32,48,256]{2,1,0:T(8,128)(2,1)S(1)} %get-tuple-element.50.refs_1_, bf16[32,96,256]{2,1,0:T(8,128)(2,1)} %copy-done.4, ...), custom_call_target="tpu_custom_call" | custom-call | flops 20 | tf_op jit(solution)/shard_map/pallas_call | solution.py:199
  75.7 1.4 %copy-done.6 = bf16[16,192,256]{2,1,0:T(8,128)(2,1)S(1)} copy-done((bf16[16,192,256]{2,1,0:T(8,128)(2,1)S(1)}, bf16[16,192,256]{2,1,0:T(8,128)(2,1)}, u32[]{:S(2)}) %copy-start.6) | copy-done | bytes 1572888
  77.1 2.9 %shard_map.104 = (bf16[8,192,256]{2,1,0:T(8,128)(2,1)S(1)}, bf16[8,48,256]{2,1,0:T(8,128)(2,1)S(1)}, bf16[8,48,256]{2,1,0:T(8,128)(2,1)S(1)}) custom-call(s32[5]{0:T(128)S(1)} %pad_add_fusion.info, bf16[8,192,256]{2,1,0:T(8,128)(2,1)S(1)} %get-tuple-element.58.top, bf16[8,192,256]{2,1,0:T(8,128)(2,1)S(1)} %get-tuple-element.59.bottom, ...), custom_call_target="tpu_custom_call" | custom-call | flops 10 | tf_op jit(solution)/shard_map/pallas_call | solution.py:199
  80.5 0.9 collective-permute-done.8.left
  81.8 4.6 %shard_map.105 = bf16[8,192,256]{2,1,0:T(8,128)(2,1)S(1)} custom-call(s32[5]{0:T(128)S(1)} %pad_add_fusion.info, s32[2]{0:T(128)S(1)} %get-tuple-element.61.base, bf16[8,48,256]{2,1,0:T(8,128)(2,1)S(1)} %collective-permute-done.8.left, bf16[8,192,256]{2,1,0:T(8,128)(2,1)S(1)} %get-tuple-element.64.middle, ...), custom_call_target="tpu_custom_call" | custom-call | flops 26 | tf_op jit(solution)/shard_map/pallas_call | solution.py:199
  86.4 1.6 %collective-permute-start.13 = (bf16[8,192,256]{2,1,0:T(8,128)(2,1)S(1)}, bf16[8,192,256]{2,1,0:T(8,128)(2,1)S(1)}, u32[]{:S(2)}, u32[]{:S(2)}) collective-permute-start(bf16[8,192,256]{2,1,0:T(8,128)(2,1)S(1)} %shard_map.105), channel_id=1, source_target_pairs={{0,2},{2,0},{4,6},{6,4},{8,10},{10,8},{12,14},{14,12},{1,3},{3,1},... | collective-permute-start | bytes 2359304 | tf_op jit(solution)/shard_map/ppermute | solution.py:246
  88.0 0.8 collective-permute-done.10.south
  88.8 6.9 %shard_map.106 = (bf16[24,192,256]{2,1,0:T(8,128)(2,1)}, bf16[24,48,256]{2,1,0:T(8,128)(2,1)S(1)}, bf16[24,48,256]{2,1,0:T(8,128)(2,1)S(1)}) custom-call(s32[5]{0:T(128)S(1)} %pad_add_fusion.info, bf16[8,192,256]{2,1,0:T(8,128)(2,1)S(1)} %get-tuple-element.58.top, bf16[8,192,256]{2,1,0:T(8,128)(2,1)S(1)} %get-tuple-element.59.bottom, ...), custom_call_target="tpu_custom_call" | custom-call | flops 30 | tf_op jit(solution)/shard_map/pallas_call | solution.py:199
  96.3 1.5 %collective-permute-done.11.left = bf16[24,48,256]{2,1,0:T(8,128)(2,1)S(1)} collective-permute-done((bf16[24,48,256]{2,1,0:T(8,128)(2,1)S(1)}, bf16[24,48,256]{2,1,0:T(8,128)(2,1)S(1)}, u32[]{:S(2)}, u32[]{:S(2)}) %collective-permute-start.11) | collective-permute-done | bytes 589856 | tf_op jit(solution)/shard_map/ppermute | solution.py:249
  97.8 0.8 collective-permute-done.12.right
  98.6 5.7 %shard_map.107 = bf16[8,192,256]{2,1,0:T(8,128)(2,1)S(1)} custom-call(s32[5]{0:T(128)S(1)} %pad_add_fusion.info, s32[2]{0:T(128)S(1)} %get-tuple-element.72.base, bf16[24,48,256]{2,1,0:T(8,128)(2,1)S(1)} %collective-permute-done.11.left, bf16[24,192,256]{2,1,0:T(8,128)(2,1)} %get-tuple-element.75.middle, ...), custom_call_target="tpu_custom_call" | custom-call | flops 26 | tf_op jit(solution)/shard_map/pallas_call | solution.py:199
  104.3 1.6 %collective-permute-start.14 = (bf16[8,192,256]{2,1,0:T(8,128)(2,1)S(1)}, bf16[8,192,256]{2,1,0:T(8,128)(2,1)S(1)}, u32[]{:S(2)}, u32[]{:S(2)}) collective-permute-start(bf16[8,192,256]{2,1,0:T(8,128)(2,1)S(1)} %shard_map.107), channel_id=1, source_target_pairs={{0,2},{2,0},{4,6},{6,4},{8,10},{10,8},{12,14},{14,12},{1,3},{3,1},... | collective-permute-start | bytes 2359304 | tf_op jit(solution)/shard_map/ppermute | solution.py:246
  106.2 5.7 %shard_map.109 = bf16[8,192,256]{2,1,0:T(8,128)(2,1)S(1)} custom-call(s32[5]{0:T(128)S(1)} %pad_add_fusion.info, s32[2]{0:T(128)S(1)} %get-tuple-element.76.base, bf16[24,48,256]{2,1,0:T(8,128)(2,1)S(1)} %collective-permute-done.11.left, bf16[24,192,256]{2,1,0:T(8,128)(2,1)} %get-tuple-element.75.middle, ...), custom_call_target="tpu_custom_call" | custom-call | flops 26 | tf_op jit(solution)/shard_map/pallas_call | solution.py:199
  111.8 5.6 %shard_map.108 = bf16[8,192,256]{2,1,0:T(8,128)(2,1)S(1)} custom-call(s32[5]{0:T(128)S(1)} %pad_add_fusion.info, s32[2]{0:T(128)S(1)} %get-tuple-element.42.base, bf16[24,48,256]{2,1,0:T(8,128)(2,1)S(1)} %collective-permute-done.11.left, bf16[24,192,256]{2,1,0:T(8,128)(2,1)} %get-tuple-element.75.middle, ...), custom_call_target="tpu_custom_call" | custom-call | flops 26 | tf_op jit(solution)/shard_map/pallas_call | solution.py:199
  118.1 5.9 %collective-permute-done.14 = bf16[8,192,256]{2,1,0:T(8,128)(2,1)S(1)} collective-permute-done((bf16[8,192,256]{2,1,0:T(8,128)(2,1)S(1)}, bf16[8,192,256]{2,1,0:T(8,128)(2,1)S(1)}, u32[]{:S(2)}, u32[]{:S(2)}) %collective-permute-start.14) | collective-permute-done | bytes 786464 | tf_op jit(solution)/shard_map/ppermute | solution.py:246
  124.0 0.9 bitcast_dynamic-update-slice_fusion
  (65 shorter events, 4.5 us)
Async XLA Ops:
  2.1 21.5 %collective-permute-start = (bf16[8,192,256]{2,1,0:T(8,128)(2,1)}, bf16[8,192,256]{2,1,0:T(8,128)(2,1)S(1)}, u32[]{:S(2)}, u32[]{:S(2)}) collective-permute-start(bf16[8,192,256]{2,1,0:T(8,128)(2,1)} %dynamic-slice_bitcast_fusion.2), channel_id=1, source_target_pairs={{0,2},{2,0},{4,6},{6,4},{8,10},{10,8},{12,14},{14,12},{1,3},{3,1},... | collective-permute-start | bytes 2359304 | tf_op jit(solution)/shard_map/ppermute | solution.py:246
  5.0 4.2 %copy-start.11 = (bf16[2,5,2,128,128]{4,3,2,1,0:T(8,128)(2,1)S(1)}, bf16[2,5,2,128,128]{4,3,2,1,0:T(8,128)(2,1)}, u32[]{:S(2)}) copy-start(bf16[2,5,2,128,128]{4,3,2,1,0:T(8,128)(2,1)} %param.12) | copy-start | bytes 1966084
  7.8 1.5 %copy-start.12 = (bf16[2,5,2,128,128]{4,3,2,1,0:T(8,128)(2,1)S(1)}, bf16[2,5,2,128,128]{4,3,2,1,0:T(8,128)(2,1)}, u32[]{:S(2)}) copy-start(bf16[2,5,2,128,128]{4,3,2,1,0:T(8,128)(2,1)} %param.13) | copy-start | bytes 1966084
  7.8 33.4 %collective-permute-start.1 = (bf16[8,192,256]{2,1,0:T(8,128)(2,1)}, bf16[8,192,256]{2,1,0:T(8,128)(2,1)}, u32[]{:S(2)}, u32[]{:S(2)}) collective-permute-start(bf16[8,192,256]{2,1,0:T(8,128)(2,1)} %get-tuple-element.78), channel_id=1, source_target_pairs={{0,2},{2,0},{4,6},{6,4},{8,10},{10,8},{12,14},{14,12},{1,3},{3,1},... | collective-permute-start | bytes 2359304 | tf_op jit(solution)/shard_map/ppermute | solution.py:246
  7.8 33.4 %collective-permute-start.3 = (bf16[8,192,256]{2,1,0:T(8,128)(2,1)}, bf16[8,192,256]{2,1,0:T(8,128)(2,1)}, u32[]{:S(2)}, u32[]{:S(2)}) collective-permute-start(bf16[8,192,256]{2,1,0:T(8,128)(2,1)} %get-tuple-element.77), channel_id=1, source_target_pairs={{4,0},{8,4},{12,8},{2,6},{6,10},{10,14},{5,1},{9,5},{13,9},{3,7},{... | collective-permute-start | bytes 2359304 | tf_op jit(solution)/shard_map/ppermute | solution.py:262
  9.5 0.7 copy-start.15
  9.5 0.7 copy-start.16
  10.3 0.7 copy-start.14
  10.3 18.2 %copy-start.13 = (s32[16,192]{1,0:T(8,128)S(1)}, s32[16,192]{1,0:T(8,128)}, u32[]{:S(2)}) copy-start(s32[16,192]{1,0:T(8,128)} %param.19) | copy-start | bytes 36868
  23.6 18.9 %collective-permute-start.4 = (bf16[8,192,256]{2,1,0:T(8,128)(2,1)S(1)}, bf16[8,192,256]{2,1,0:T(8,128)(2,1)}, u32[]{:S(2)}, u32[]{:S(2)}) collective-permute-start(bf16[8,192,256]{2,1,0:T(8,128)(2,1)S(1)} %collective-permute-done.edge), channel_id=1, source_target_pairs={{0,4},{4,8},{8,12},{6,2},{10,6},{14,10},{1,5},{5,9},{9,13},{7,3},{... | collective-permute-start | bytes 2359304 | tf_op jit(solution)/shard_map/ppermute | solution.py:281
  28.5 11.5 %collective-permute-start.2 = (f32[16,192]{1,0:T(8,128)S(1)}, f32[16,192]{1,0:T(8,128)S(1)}, u32[]{:S(2)}, u32[]{:S(2)}) collective-permute-start(f32[16,192]{1,0:T(8,128)S(1)} %convert_element_type.3), channel_id=1, source_target_pairs={{0,2},{2,0},{4,6},{6,4},{8,10},{10,8},{12,14},{14,12},{1,3},{3,1},... | collective-permute-start | bytes 36872 | tf_op jit(solution)/shard_map/ppermute | solution.py:246
  47.7 0.9 copy-start.7
  48.6 7.8 %collective-permute-start.5 = (bf16[32,48,256]{2,1,0:T(8,128)(2,1)S(1)}, bf16[32,48,256]{2,1,0:T(8,128)(2,1)S(1)}, u32[]{:S(2)}, u32[]{:S(2)}) collective-permute-start(bf16[32,48,256]{2,1,0:T(8,128)(2,1)S(1)} %get-tuple-element.49.refs_3_), channel_id=1, source_target_pairs={{0,1},{1,0},{2,3},{3,2},{4,5},{5,4},{6,7},{7,6},{8,9},{9,8},{10,11... | collective-permute-start | bytes 2359304 | tf_op jit(solution)/shard_map/ppermute | solution.py:249
  48.6 7.8 %collective-permute-start.6 = (bf16[32,48,256]{2,1,0:T(8,128)(2,1)S(1)}, bf16[32,48,256]{2,1,0:T(8,128)(2,1)S(1)}, u32[]{:S(2)}, u32[]{:S(2)}) collective-permute-start(bf16[32,48,256]{2,1,0:T(8,128)(2,1)S(1)} %get-tuple-element.50.refs_1_), channel_id=1, source_target_pairs={{1,0},{0,1},{3,2},{2,3},{5,4},{4,5},{7,6},{6,7},{9,8},{8,9},{11,10... | collective-permute-start | bytes 2359304 | tf_op jit(solution)/shard_map/ppermute | solution.py:249
  55.3 1.2 copy-start.4
  56.5 12.7 %copy-start = (f32[8,4,192]{1,2,0:T(8,128)S(1)}, f32[8,4,192]{1,2,0:T(8,128)}, u32[]{:S(2)}) copy-start(f32[8,4,192]{1,2,0:T(8,128)} %copy.19) | copy-start | bytes 73732
  56.5 12.7 %copy-start.8 = (bf16[32,48,256]{2,1,0:T(8,128)(2,1)S(1)}, bf16[32,48,256]{2,1,0:T(8,128)(2,1)}, u32[]{:S(2)}) copy-start(bf16[32,48,256]{2,1,0:T(8,128)(2,1)} %copy-done.7) | copy-start | bytes 2359300
  63.1 24.9 %collective-permute-start.7 = (bf16[8,192,256]{2,1,0:T(8,128)(2,1)S(1)}, bf16[8,192,256]{2,1,0:T(8,128)(2,1)S(1)}, u32[]{:S(2)}, u32[]{:S(2)}) collective-permute-start(bf16[8,192,256]{2,1,0:T(8,128)(2,1)S(1)} %get-tuple-element.59.bottom), channel_id=1, source_target_pairs={{0,4},{2,6},{4,8},{6,10},{8,12},{10,14},{1,5},{3,7},{5,9},{7,11},{... | collective-permute-start | bytes 2359304 | tf_op jit(solution)/shard_map/ppermute | solution.py:385
  67.7 21.2 %collective-permute-start.10 = (bf16[8,192,256]{2,1,0:T(8,128)(2,1)S(1)}, bf16[8,192,256]{2,1,0:T(8,128)(2,1)}, u32[]{:S(2)}, u32[]{:S(2)}) collective-permute-start(bf16[8,192,256]{2,1,0:T(8,128)(2,1)S(1)} %get-tuple-element.58.top), channel_id=1, source_target_pairs={{4,0},{6,2},{8,4},{10,6},{12,8},{14,10},{5,1},{7,3},{9,5},{11,7},{... | collective-permute-start | bytes 2359304 | tf_op jit(solution)/shard_map/ppermute | solution.py:386
  75.7 1.4 %copy-start.6 = (bf16[16,192,256]{2,1,0:T(8,128)(2,1)S(1)}, bf16[16,192,256]{2,1,0:T(8,128)(2,1)}, u32[]{:S(2)}) copy-start(bf16[16,192,256]{2,1,0:T(8,128)(2,1)} %get-tuple-element.60.inner) | copy-start | bytes 4718596
  77.1 4.7 %copy-start.1 = (bf16[256,1024]{1,0:T(8,128)(2,1)S(1)}, bf16[256,1024]{1,0:T(8,128)(2,1)}, u32[]{:S(2)}) copy-start(bf16[256,1024]{1,0:T(8,128)(2,1)} %w_in.7) | copy-start | bytes 1572868
  77.1 4.7 %copy-start.2 = (bf16[1024,256]{1,0:T(8,128)(2,1)S(1)}, bf16[1024,256]{1,0:T(8,128)(2,1)}, u32[]{:S(2)}) copy-start(bf16[1024,256]{1,0:T(8,128)(2,1)} %w_out.7) | copy-start | bytes 1572868
  77.1 4.7 %copy-start.5 = (bf16[16,192,256]{2,1,0:T(8,128)(2,1)S(1)}, bf16[16,192,256]{2,1,0:T(8,128)(2,1)}, u32[]{:S(2)}) copy-start(bf16[16,192,256]{2,1,0:T(8,128)(2,1)} %get-tuple-element.66.state) | copy-start | bytes 4718596
  77.1 4.7 %copy-start.9 = (f32[256]{0:T(256)S(1)}, f32[256]{0:T(256)}, u32[]{:S(2)}) copy-start(f32[256]{0:T(256)} %param.14) | copy-start | bytes 3076
  80.0 1.5 %collective-permute-start.8 = (bf16[8,48,256]{2,1,0:T(8,128)(2,1)S(1)}, bf16[8,48,256]{2,1,0:T(8,128)(2,1)S(1)}, u32[]{:S(2)}, u32[]{:S(2)}) collective-permute-start(bf16[8,48,256]{2,1,0:T(8,128)(2,1)S(1)} %get-tuple-element.63), channel_id=1, source_target_pairs={{0,1},{1,0},{2,3},{3,2},{4,5},{5,4},{6,7},{7,6},{8,9},{9,8},{10,11... | collective-permute-start | bytes 589832 | tf_op jit(solution)/shard_map/ppermute | solution.py:249
  80.0 1.7 %collective-permute-start.9 = (bf16[8,48,256]{2,1,0:T(8,128)(2,1)S(1)}, bf16[8,48,256]{2,1,0:T(8,128)(2,1)S(1)}, u32[]{:S(2)}, u32[]{:S(2)}) collective-permute-start(bf16[8,48,256]{2,1,0:T(8,128)(2,1)S(1)} %get-tuple-element.65), channel_id=1, source_target_pairs={{1,0},{0,1},{3,2},{2,3},{5,4},{4,5},{7,6},{6,7},{9,8},{8,9},{11,10... | collective-permute-start | bytes 589832 | tf_op jit(solution)/shard_map/ppermute | solution.py:249
  86.4 12.2 %copy-start.3 = (bf16[16,192,256]{2,1,0:T(8,128)(2,1)S(1)}, bf16[16,192,256]{2,1,0:T(8,128)(2,1)}, u32[]{:S(2)}) copy-start(bf16[16,192,256]{2,1,0:T(8,128)(2,1)} %get-tuple-element.74.state) | copy-start | bytes 4718596
  86.4 19.7 %collective-permute-start.13 = (bf16[8,192,256]{2,1,0:T(8,128)(2,1)S(1)}, bf16[8,192,256]{2,1,0:T(8,128)(2,1)S(1)}, u32[]{:S(2)}, u32[]{:S(2)}) collective-permute-start(bf16[8,192,256]{2,1,0:T(8,128)(2,1)S(1)} %shard_map.105), channel_id=1, source_target_pairs={{0,2},{2,0},{4,6},{6,4},{8,10},{10,8},{12,14},{14,12},{1,3},{3,1},... | collective-permute-start | bytes 2359304 | tf_op jit(solution)/shard_map/ppermute | solution.py:246
  95.8 2.0 %collective-permute-start.11 = (bf16[24,48,256]{2,1,0:T(8,128)(2,1)S(1)}, bf16[24,48,256]{2,1,0:T(8,128)(2,1)S(1)}, u32[]{:S(2)}, u32[]{:S(2)}) collective-permute-start(bf16[24,48,256]{2,1,0:T(8,128)(2,1)S(1)} %get-tuple-element.70), channel_id=1, source_target_pairs={{0,1},{1,0},{2,3},{3,2},{4,5},{5,4},{6,7},{7,6},{8,9},{9,8},{10,11... | collective-permute-start | bytes 1769480 | tf_op jit(solution)/shard_map/ppermute | solution.py:249
  95.8 2.8 %collective-permute-start.12 = (bf16[24,48,256]{2,1,0:T(8,128)(2,1)S(1)}, bf16[24,48,256]{2,1,0:T(8,128)(2,1)S(1)}, u32[]{:S(2)}, u32[]{:S(2)}) collective-permute-start(bf16[24,48,256]{2,1,0:T(8,128)(2,1)S(1)} %get-tuple-element.73), channel_id=1, source_target_pairs={{1,0},{0,1},{3,2},{2,3},{5,4},{4,5},{7,6},{6,7},{9,8},{8,9},{11,10... | collective-permute-start | bytes 1769480 | tf_op jit(solution)/shard_map/ppermute | solution.py:249
  104.3 19.6 %collective-permute-start.14 = (bf16[8,192,256]{2,1,0:T(8,128)(2,1)S(1)}, bf16[8,192,256]{2,1,0:T(8,128)(2,1)S(1)}, u32[]{:S(2)}, u32[]{:S(2)}) collective-permute-start(bf16[8,192,256]{2,1,0:T(8,128)(2,1)S(1)} %shard_map.107), channel_id=1, source_target_pairs={{0,2},{2,0},{4,6},{6,4},{8,10},{10,8},{12,14},{14,12},{1,3},{3,1},... | collective-permute-start | bytes 2359304 | tf_op jit(solution)/shard_map/ppermute | solution.py:246
  118.0 5.9 %copy-start.10 = (bf16[2,16,192,256]{3,2,1,0:T(8,128)(2,1)}, bf16[2,16,192,256]{3,2,1,0:T(8,128)(2,1)S(1)}, u32[]{:S(2)}) copy-start(bf16[2,16,192,256]{3,2,1,0:T(8,128)(2,1)S(1)} %bitcast_dynamic-update-slice_fusion.1) | copy-start | bytes 9437188
